TPU v7x, 256 devices: a whole 4x4x8 slice. The times are simulated.
256 devices in a mesh: replica: 16 (over y_lo, z), shard: 16 (over y_hi, x, core).
Axes of the slice: x: 4, y: 4 (y_hi: 2, y_lo: 2; y = y_hi * 2 + y_lo), z: 8, core: 2. Of those that a mesh axis runs over, the one named last changes fastest.
Arguments:
- grads: bfloat16 [16, 3072, 8192], P('replica', 'shard'), may hold values from -6 to 6
- errors: bfloat16 [16, 3072, 8192], P('replica', 'shard'), may hold values from -4 to 4
- basis: bfloat16 [3072, 512], P('shard'), may hold values from -0.109375 to 0.109375
- params: float32 [3072, 8192], P('replica', 'shard'), may hold values from -6 to 6
- momentum: float32 [3072, 8192], P('replica', 'shard'), may hold values from -1.2 to 1.2
Outputs:
- new_params: float32 [3072, 8192], P('replica', 'shard')
- new_momentum: float32 [3072, 8192], P('replica', 'shard')
- new_errors: bfloat16 [16, 3072, 8192], P('replica', 'shard')
All inputs are finite; a program needn't handle non-finite values.
Results may differ from a plain program's by a relative error of at most 0.012.
Values may be sent and summed in bfloat16 or wider, within the bound.
A program may use at most 128 MiB of HBM per device.

v0:
```python
import jax
import jax.numpy as jnp
from jax import lax
from jax.sharding import PartitionSpec as P

momentum_rate = 0.9
outer_rate = 0.7


def padded_to(lines, size):
    spare = -lines.shape[0] % size
    if not spare:
        return lines
    return jnp.concatenate([lines, jnp.zeros((spare, *lines.shape[1:]), lines.dtype)])


def copy_for_each(array, axis):
    size = lax.axis_size(axis)
    return lax.all_to_all(
        jnp.broadcast_to(array[None], (size, *array.shape)), axis, 0, 0, tiled=True
    )


def laid_out(tiles, dim):
    shape = list(tiles.shape[1:])
    shape[dim] *= tiles.shape[0]
    return jnp.moveaxis(tiles, 0, dim).reshape(shape)


def gathered_copies(array, axis, dim):
    tiles = copy_for_each(array, axis)
    return laid_out(tiles, dim)


def cut_along(array, dim, size):
    shape = array.shape
    tiles = array.reshape(*shape[:dim], size, shape[dim] // size, *shape[dim + 1 :])
    return jnp.moveaxis(tiles, dim, 0)


def sum_at_owner(array, axis, dim):
    tiles = cut_along(array, dim, lax.axis_size(axis))
    arrived = lax.all_to_all(tiles, axis, split_axis=0, concat_axis=0, tiled=True)
    return arrived.astype(jnp.float32).sum(axis=0)


def total_of(array, axes):
    lines = array.reshape(-1, array.shape[-1])
    padded = padded_to(lines, lax.axis_size(axes))
    whole = gathered_copies(sum_at_owner(padded, axes, 0).astype(jnp.bfloat16), axes, 0)
    return lax.slice_in_dim(whole, 0, len(lines)).reshape(array.shape).astype(jnp.float32)


def body(grads, errors, basis, params, momentum):
    corrected = (grads[0].astype(jnp.float32) + errors[0].astype(jnp.float32)).astype(jnp.bfloat16)
    shards = lax.axis_size("shard")
    column_span = corrected.shape[1] // shards
    basis_full = lax.all_gather(basis, "shard", axis=0, tiled=True)
    column_block = lax.all_to_all(corrected, "shard", split_axis=1, concat_axis=0, tiled=True)
    block_rows = corrected.shape[0]
    stacked = column_block.reshape(shards, block_rows, column_span)
    basis_stack = basis_full.reshape(shards, block_rows, basis_full.shape[1])
    partials = jnp.einsum("nrc,nrk->nck", stacked, basis_stack, preferred_element_type=jnp.float32)
    coeff_piece = jnp.sum(partials.astype(jnp.bfloat16).astype(jnp.float32), axis=0).astype(
        jnp.bfloat16
    )
    rebuilt_cols = lax.dot_general(
        basis_full, coeff_piece, (((1,), (1,)), ((), ())), preferred_element_type=jnp.float32
    )
    error_cols = (column_block.astype(jnp.float32) - rebuilt_cols).astype(jnp.bfloat16)
    new_error = lax.all_to_all(error_cols, "shard", split_axis=0, concat_axis=1, tiled=True)
    replicas = lax.axis_size("replica")
    summed = total_of(coeff_piece.astype(jnp.float32).astype(jnp.bfloat16), "replica")
    mean_piece = (summed * (1.0 / replicas)).astype(jnp.bfloat16)
    own_rows = params.shape[0]
    basis_own = lax.dynamic_slice_in_dim(
        basis_full, lax.axis_index("replica") * own_rows, own_rows, 0
    )
    outer_grad = lax.dot_general(
        basis_own, mean_piece, (((1,), (1,)), ((), ())), preferred_element_type=jnp.float32
    )
    new_momentum = momentum_rate * momentum + outer_grad
    new_params = params - outer_rate * (outer_grad + momentum_rate * new_momentum)
    return (new_params, new_momentum, new_error[None])


def solution(mesh):
    in_specs = (
        P("replica", "shard", None),
        P("replica", "shard", None),
        P("shard", None),
        P("replica", "shard"),
        P("replica", "shard"),
    )
    out_specs = (P("replica", "shard"), P("replica", "shard"), P("replica", "shard", None))
    return jax.shard_map(body, mesh=mesh, in_specs=in_specs, out_specs=out_specs, check_vma=False)
```

profile of v0, /device:TPU:1, one launch (start us, length us, event | category | flops | bytes accessed | tf_op | source)
XLA Modules:
  0.0 200.0 jit_solution(15753682389976008219)
XLA Ops:
  7.2 0.0 all-gather.2.cloned.1.call-start
  7.2 0.7 all-gather.2.cloned.1.call-update
  7.9 3.9 %add_convert_fusion = bf16[1,192,8192]{2,1,0:T(8,128)(2,1)S(1)} fusion(bf16[1,192,8192]{2,1,0:T(8,128)(2,1)} %param.6, bf16[1,192,8192]{2,1,0:T(8,128)(2,1)} %param.5), kind=kLoop, calls=%fused_computation.3 | loop fusion | flops 6291456 | bytes 9437184 | tf_op jit(solution)/shard_map/convert_element_type | solution.py:55
  11.8 1.3 copy.21
  13.2 1.8 copy.17
  14.9 50.9 %all_to_all.39 = bf16[192,16,512]{2,0,1:T(8,128)(2,1)S(1)} all-to-all(bf16[192,16,512]{2,0,1:T(8,128)(2,1)S(1)} %copy.17), channel_id=1, replica_groups=mesh['replica'=16,'shard'=16] {'shard'}, dimensions={1} | all-to-all | bytes 6291456 | tf_op jit(solution)/shard_map/all_to_all | solution.py:59
  65.8 16.3 %all-gather.2.cloned.1.call-done = bf16[3072,512]{1,0:T(8,128)(2,1)} async-done(((bf16[192,512]{1,0:T(8,128)(2,1)}), bf16[3072,512]{1,0:T(8,128)(2,1)}) %all-gather.2.cloned.1.call-update) | async-done | bytes 3145744 | tf_op jit(solution)/shard_map/all_gather | solution.py:58
  82.1 4.4 %convert_reduce_fusion = bf16[512,512]{1,0:T(8,128)(2,1)S(1)} fusion(bf16[16,192,512]{2,1,0:T(8,128)(2,1)} %bitcast.26, bf16[192,16,512]{2,0,1:T(8,128)(2,1)S(1)} %all_to_all.39), kind=kOutput, calls=%fused_computation | convolution fusion | flops 1618739200 | bytes 6815744 | tf_op jit(solution)/shard_map/nrc,nrk->nck/dot_general | solution.py:63
  86.5 0.0 copy-start
  86.5 0.8 copy-done
  87.3 21.4 %all_to_all.40 = bf16[16,32,512]{2,1,0:T(8,128)(2,1)} all-to-all(bf16[16,32,512]{2,1,0:T(8,128)(2,1)S(1)} %bitcast.27), channel_id=1, replica_groups=mesh['replica'=16,'shard'=16] {'replica'}, dimensions={0} | all-to-all | bytes 1048576 | tf_op jit(solution)/shard_map/all_to_all | solution.py:43
  108.6 1.1 reduce_sum.25
  109.7 0.9 broadcast_in_dim.4
  110.6 6.8 %all-to-all-start.2 = ((bf16[16,32,512]{2,1,0:T(8,128)(2,1)}), bf16[16,32,512]{2,1,0:T(8,128)(2,1)}, u32[]{:S(2)}, u32[]{:S(2)}) async-start(bf16[16,32,512]{2,1,0:T(8,128)(2,1)} %broadcast_in_dim.4), calls=%async_computation.2 | async-start | bytes 1048576 | tf_op jit(solution)/shard_map/all_to_all | solution.py:19
  117.4 3.8 %bitcast_convert_fusion = f32[3072,512]{1,0:T(8,128)} fusion(bf16[192,16,512]{2,0,1:T(8,128)(2,1)S(1)} %all_to_all.39), kind=kLoop, calls=%fused_computation.4 | loop fusion | flops 1572864 | bytes 9437184 | tf_op jit(solution)/shard_map/convert_element_type | solution.py:70
  121.1 6.5 %copy.18 = f32[3072,512]{0,1:T(8,128)} copy(f32[3072,512]{1,0:T(8,128)} %bitcast_convert_fusion) | data formatting | bytes 12582912 | tf_op jit(solution)/shard_map/convert_element_type | solution.py:70
  127.7 5.7 %fusion = bf16[3072,512]{0,1:T(8,128)(2,1)S(1)} fusion(f32[3072,512]{0,1:T(8,128)} %copy.18, bf16[512,512]{1,0:T(8,128)(2,1)} %copy-done, bf16[3072,512]{1,0:T(8,128)(2,1)} %all-gather.2.cloned.1.call-done), kind=kOutput, calls=%fused_computation.2 | convolution fusion | flops 1613758464 | bytes 13107200 | tf_op jit(solution)/shard_map/dot_general | solution.py:67
  133.4 2.8 %copy.19 = bf16[3072,512]{1,0:T(8,128)(2,1)} copy(bf16[3072,512]{0,1:T(8,128)(2,1)S(1)} %fusion) | data formatting | bytes 6291456 | tf_op jit(solution)/shard_map/convert_element_type | solution.py:70
  136.2 0.0 all-to-all-done.2
  136.2 0.0 copy-start.1
  136.2 5.8 %all-to-all-start.3 = ((bf16[16,192,512]{2,1,0:T(8,128)(2,1)}), bf16[16,192,512]{2,1,0:T(8,128)(2,1)S(1)}, u32[]{:S(2)}, u32[]{:S(2)}) async-start(bf16[16,192,512]{2,1,0:T(8,128)(2,1)} %bitcast.6), calls=%async_computation.3 | async-start | bytes 6291456 | tf_op jit(solution)/shard_map/all_to_all | solution.py:71
  142.0 1.1 multiply_convert_fusion
  143.2 0.0 copy-done.1
  143.2 2.3 %multiply_subtract_fusion = (f32[192,512]{1,0:T(8,128)}, f32[192,512]{1,0:T(8,128)}) fusion(f32[192,512]{1,0:T(8,128)S(1)} %copy-done.1, f32[192,512]{1,0:T(8,128)} %param.9, bf16[512,512]{1,0:T(8,128)(2,1)S(1)} %bitcast.28, bf16[3072,512]{1,0:T(8,128)(2,1)} %all-gather.2.cloned.1.call-done, s32[]{:T(128)S(6)} %select_n.3), kind=kOutput, calls=%fused_computation.7 | convolution fusion | flops 101253120 | bytes 2293764 | tf_op jit(solution)/shard_map/dot_general | solution.py:79
  145.5 38.4 %all-to-all-done.3 = bf16[16,192,512]{2,1,0:T(8,128)(2,1)S(1)} async-done(((bf16[16,192,512]{2,1,0:T(8,128)(2,1)}), bf16[16,192,512]{2,1,0:T(8,128)(2,1)S(1)}, u32[]{:S(2)}, u32[]{:S(2)}) %all-to-all-start.3) | async-done | bytes 3145760 | tf_op jit(solution)/shard_map/all_to_all | solution.py:71
  183.9 3.4 %copy.20 = bf16[192,16,512]{2,1,0:T(8,128)(2,1)} copy(bf16[192,16,512]{2,0,1:T(8,128)(2,1)S(1)} %bitcast.23) | data formatting | bytes 6291456 | tf_op jit(solution)/shard_map/all_to_all | solution.py:71
  187.3 5.9 %broadcast_in_dim.10 = bf16[1,192,8192]{2,1,0:T(8,128)(2,1)} reshape(bf16[192,16,512]{2,1,0:T(8,128)(2,1)} %copy.20) | data formatting | bytes 6291456 | tf_op jit(solution)/shard_map/broadcast_in_dim | solution.py:84
Async XLA Ops:
  7.2 74.9 %all-gather.2.cloned.1.call-start = ((), (), s32[]{:S(2)}) async-start(), calls=%async_computation.4 | async-start | bytes 3342336 | tf_op jit(solution)/shard_map/all_gather | solution.py:58
  86.5 0.8 copy-start
  110.6 25.6 %all-to-all-start.2 = ((bf16[16,32,512]{2,1,0:T(8,128)(2,1)}), bf16[16,32,512]{2,1,0:T(8,128)(2,1)}, u32[]{:S(2)}, u32[]{:S(2)}) async-start(bf16[16,32,512]{2,1,0:T(8,128)(2,1)} %broadcast_in_dim.4), calls=%async_computation.2 | async-start | bytes 1048576 | tf_op jit(solution)/shard_map/all_to_all | solution.py:19
  136.2 7.0 %copy-start.1 = (f32[192,512]{1,0:T(8,128)S(1)}, f32[192,512]{1,0:T(8,128)}, u32[]{:S(2)}) copy-start(f32[192,512]{1,0:T(8,128)} %param.8) | copy-start | bytes 1179652
  136.2 47.7 %all-to-all-start.3 = ((bf16[16,192,512]{2,1,0:T(8,128)(2,1)}), bf16[16,192,512]{2,1,0:T(8,128)(2,1)S(1)}, u32[]{:S(2)}, u32[]{:S(2)}) async-start(bf16[16,192,512]{2,1,0:T(8,128)(2,1)} %bitcast.6), calls=%async_computation.3 | async-start | bytes 6291456 | tf_op jit(solution)/shard_map/all_to_all | solution.py:71
Sparse Core Ops, SparseCore 0:
  10.7 71.3 all-gather.1
where the time goes:
time: 201 us; the launch traced here: 200 us
  blocking collectives  72.2 us (36%)
  waiting for transfers between devices  55.3 us (28%)
  local copies, waits for them, and re-layouts  23.3 us (12%)
  between operations  14.1 us (7%)
  starting transfers between devices  12.6 us (6%)
  matrix products  12.5 us (6%)
  other arithmetic  9.92 us (5%)
    all_to_all x1, blocking collectives, body(): lax.all_to_all(corrected, 'shard', split_axis=1, concat_axis=0, tiled=True)  50.9 us
    all_to_all x1, waiting for transfers between devices, body(): lax.all_to_all(error_cols, 'shard', split_axis=0, concat_axis=1, tiled=True)  38.4 us
    all_to_all x1, blocking collectives, sum_at_owner(): lax.all_to_all(tiles, axis, split_axis=0, concat_axis=0, tiled=True)  21.4 us
    all_gather x1, waiting for transfers between devices, body(): basis_full = lax.all_gather(basis, 'shard', axis=0, tiled=True)  16.3 us
    all_to_all x1, starting transfers between devices, copy_for_each(): lax.all_to_all(jnp.broadcast_to(array[None], (size, *array.shape)), axis,...  6.79 us
    convert_element_type x1, local copies, waits for them, and re-layouts, body(): column_block.astype(jnp.float32) - rebuilt_cols  6.53 us
    broadcast_in_dim x1, local copies, waits for them, and re-layouts, body(): return (new_params, new_momentum, new_error[None])  5.85 us
    all_to_all x1, starting transfers between devices, body(): lax.all_to_all(error_cols, 'shard', split_axis=0, concat_axis=1, tiled=True)  5.82 us
  transfers between devices with their start and end apart: 3, of which 2 were waited for; matrix products, arithmetic and copies ran while one was open for 15% of the time, Pallas kernels for 0%

commit v1 on v0

v1 whole, which is shorter than its diff:
```python
import jax
import jax.numpy as jnp
from jax import lax
from jax.experimental import pallas as pl
from jax.experimental.pallas import tpu as pltpu
from jax.sharding import PartitionSpec as P

momentum_rate = 0.9
outer_rate = 0.7
MESH = pl.DeviceIdType.MESH
F32, BF16 = jnp.float32, jnp.bfloat16

Y_FIRST = (True, True)
STAGES = 2
ROWS, RANK, LANES = 192, 512, 128


def kernel(g, e, b, o, og, ge, sb, cb, bb, bt, ps, kp, pr, xs, xr, cf, er, rep, rz, ys, yr, mean, bown,
           ldsem, bsem_s, bsem_r, s1, r1, s2, r2, s3, r3, s5, r5, s6, r6, zs, zr, ysm, yrm, as_, ar, osem, lsem):
    shard, replica = lax.axis_index("shard"), lax.axis_index("replica")
    yh, x, c = shard // 8, lax.rem(shard // 2, 4), lax.rem(shard, 2)
    yl, z = replica // 8, lax.rem(replica, 8)
    par = lax.rem(x, 2)
    na = x + 1 - 2 * par
    nb = lax.rem(x + 3 + 2 * par, 4)

    def at(yh_=None, x_=None, c_=None, yl_=None, z_=None):
        yh_ = yh if yh_ is None else yh_
        x_ = x if x_ is None else x_
        c_ = c if c_ is None else c_
        yl_ = yl if yl_ is None else yl_
        z_ = z if z_ is None else z_
        return (yl_ * 8 + z_, (yh_ * 4 + x_) * 2 + c_)

    def remote(src, dst, ss, rs, dev):
        return pltpu.make_async_remote_copy(
            src_ref=src, dst_ref=dst, send_sem=ss, recv_sem=rs, device_id=dev, device_id_type=MESH)

    def nd(h):
        return na + h * (nb - na)

    def xp(h):
        return nb + h * (na - nb)

    def member(h, m):
        return at(x_=x if m < 2 else nd(h), c_=c if m % 2 == 0 else 1 - c)

    def pos(h, m):
        return lax.rem(m + 2 * (1 - h), 4)

    def rows_of(h, m):
        return pl.ds(pl.multiple_of(pos(h, m) * ROWS, ROWS), ROWS)

    def my_maj(k, m=0):
        if Y_FIRST[k]:
            return yh
        return par if m < 2 else 1 - par

    def my_min(k):
        return par if Y_FIRST[k] else yh

    def column(k, h, m, maj, mn):
        x_d = x if m < 2 else nd(h)
        x_p = xp(h) if m < 2 else lax.rem(x + 2, 4)
        c_d = c if m % 2 == 0 else 1 - c
        y_o, q = (maj, mn) if Y_FIRST[k] else (mn, maj)
        x_o = x_d + (x_p - x_d) * lax.rem(lax.rem(x_d, 2) + q, 2)
        start = ((y_o * 4 + x_o) * 2 + c_d) * 512 + h * 256 + k * LANES
        return pl.ds(pl.multiple_of(start, LANES), LANES)

    def p1(k, h):
        return at(yh_=1 - yh) if Y_FIRST[k] else at(x_=xp(h))

    def p2(k, h):
        return at(x_=xp(h)) if Y_FIRST[k] else at(yh_=1 - yh)

    def halves(body):
        def step(h, carry):
            body(h)
            return carry
        lax.fori_loop(0, 2, step, 0)

    barrier = pltpu.get_barrier_semaphore()
    partners = [at(c_=1 - c), at(x_=na), at(x_=na, c_=1 - c), at(x_=nb), at(x_=nb, c_=1 - c), at(yh_=1 - yh),
                at(yl_=1 - yl)] + [at(z_=lax.rem(z + d, 8)) for d in range(1, 8)]
    for p in partners:
        pl.semaphore_signal(barrier, inc=1, device_id=p, device_id_type=MESH)
    off_diagonal = shard != replica

    @pl.when(off_diagonal)
    def _():
        pl.semaphore_signal(barrier, inc=1, device_id=(shard, replica), device_id_type=MESH)

    own_b = pltpu.make_async_copy(b, bb.at[pl.ds(2 * ROWS, ROWS)], lsem.at[0])
    own_b.start()
    order = (2, 3, 1, 0)

    def maj_of(k, m, s):
        return lax.rem(my_maj(k, m) + 1 + s, 2)

    def load(k, s):
        for m in order:
            def one(h):
                maj = maj_of(k, m, s)
                for mn in range(2):
                    cols = column(k, h, m, maj, mn)
                    for w, src in enumerate((g, e)):
                        pltpu.make_async_copy(
                            src.at[0, :, cols], ge.at[k, h, m, maj, w, :, pl.ds(mn * LANES, LANES)],
                            ldsem.at[k, h, m, maj]).start()
            halves(one)

    def correct(k, s):
        for m in order:
            def one(h):
                maj = maj_of(k, m, s)
                piece = ge.at[k, h, m, maj]
                pltpu.make_async_copy(piece, piece, ldsem.at[k, h, m, maj]).wait()
                val = (ge[k, h, m, maj, 0].astype(F32) + ge[k, h, m, maj, 1].astype(F32)).astype(BF16)
                if m == 0:
                    cb[k, h, maj, rows_of(h, 0), :] = val
                else:
                    sb[k, h, m - 1, maj] = val
                    send1(k, h, m, maj).start()
            halves(one)

    def send1(k, h, m, maj):
        return remote(sb.at[k, h, m - 1, maj], cb.at[k, h, maj, rows_of(h, m)],
                      s1.at[k, h, m - 1, maj], r1.at[k, h, m - 1, maj], member(h, m))

    for k in range(STAGES):
        for s in range(2):
            load(k, s)

    pl.semaphore_wait(barrier, len(partners) + jnp.where(off_diagonal, 1, 0))

    def slot(i):
        return bb.at[pl.ds(i * ROWS, ROWS)]

    own_b.wait()
    basis_sends = [
        remote(slot(2), slot(0), bsem_s.at[0], bsem_r.at[0], at(x_=na)),
        remote(slot(2), slot(4), bsem_s.at[1], bsem_r.at[1], at(x_=nb)),
        remote(slot(2), slot(3), bsem_s.at[2], bsem_r.at[2], at(c_=1 - c)),
        remote(slot(0), slot(1), bsem_s.at[3], bsem_r.at[3], at(c_=1 - c)),
        remote(slot(4), slot(5), bsem_s.at[4], bsem_r.at[4], at(c_=1 - c)),
    ]
    for cp in basis_sends[:3]:
        cp.start()

    correct(0, 0)
    correct(1, 0)
    for i in range(2):
        basis_sends[i].wait_recv()
        basis_sends[3 + i].start()
    correct(0, 1)
    correct(1, 1)

    own_rows = remote(slot(2), bown, bsem_s.at[5], bsem_r.at[5], (shard, replica))
    own_rows_here = pltpu.make_async_copy(slot(2), bown, lsem.at[1])

    @pl.when(off_diagonal)
    def _():
        own_rows.start()

    @pl.when(shard == replica)
    def _():
        own_rows_here.start()

    for i in range(2, 5):
        basis_sends[i].wait_recv()

    def turn(i, carry):
        bt[:, pl.ds(pl.multiple_of(i * 2 * ROWS, 128), 2 * ROWS)] = bb[pl.ds(pl.multiple_of(i * 2 * ROWS, 128), 2 * ROWS), :].T
        return carry
    lax.fori_loop(0, 3, turn, 0)

    def send2(k, h):
        return remote(ps.at[k, h], pr.at[k, h], s2.at[k, h], r2.at[k, h], p1(k, h))

    def partial(k, s):
        def one(h):
            maj = maj_of(k, 0, s)
            for m in range(1, 4):
                send1(k, h, m, maj).wait_recv()

            def tile(i, carry):
                rk = pl.ds(pl.multiple_of(i * 256, 256), 256)
                val = jnp.dot(bt[rk, pl.ds(pl.multiple_of(h * 2 * ROWS, 128), 4 * ROWS)], cb[k, h, maj],
                              preferred_element_type=F32)
                if s == 0:
                    ps[k, h, rk, :] = val.astype(BF16)
                else:
                    kp[k, h, rk, :] = val
                return carry
            lax.fori_loop(0, 2, tile, 0)
            if s == 0:
                send2(k, h).start()
        halves(one)

    def send3(k, h):
        return remote(xs.at[k, h], xr.at[k, h], s3.at[k, h], r3.at[k, h], p2(k, h))

    def exchange(k):
        def one(h):
            send2(k, h).wait_recv()
            xs[k, h] = (kp[k, h] + pr[k, h].astype(F32)).astype(BF16)
            send3(k, h).start()
        halves(one)

    def send5(k, h):
        return remote(cf.at[k, h, my_maj(k)], cf.at[k, h, my_maj(k)], s5.at[k, h], r5.at[k, h], p1(k, h))

    def zsend(k, d):
        to = lax.rem(z + d, 8)
        return remote(rep.at[k, to], rz.at[k, d], zs.at[k, d], zr.at[k, d], at(z_=to))

    def coefficients(k):
        def one(h):
            send3(k, h).wait_recv()
            cf[k, h, my_maj(k)] = (xs[k, h].astype(F32) + xr[k, h].astype(F32)).astype(BF16)
            send5(k, h).start()
            mine = cf[k, h, my_maj(k), :, pl.ds(pl.multiple_of(my_min(k) * LANES, LANES), LANES)]
            rep[k, :, h] = mine.reshape(8, 64, LANES)
        halves(one)
        for d in range(1, 8):
            zsend(k, d).start()

    def send6(k, h, m, maj, mn):
        src = er.at[k, h, maj, rows_of(h, m), pl.ds(mn * LANES, LANES)]
        dst = o.at[0, :, column(k, h, 0, maj, mn)]
        return remote(src, dst, s6.at[k, h, m - 1, maj, mn], r6.at[k, h, m - 1, maj, mn], member(h, m))

    def keep6(k, h, maj, mn):
        src = er.at[k, h, maj, rows_of(h, 0), pl.ds(mn * LANES, LANES)]
        return pltpu.make_async_copy(src, o.at[0, :, column(k, h, 0, maj, mn)], osem.at[k, h, maj, mn])

    def receive6(k, h, m, maj, mn):
        src = er.at[k, h, maj, rows_of(h, m), pl.ds(mn * LANES, LANES)]
        dst = o.at[0, :, column(k, h, m, maj, mn)]
        return remote(src, dst, s6.at[k, h, m - 1, maj, mn], r6.at[k, h, m - 1, maj, mn], member(h, m))

    def rebuild(k, s):
        def one(h):
            maj = lax.rem(my_maj(k) + s, 2)
            if s == 1:
                send5_other(k, h).wait_recv()
            for pair in range(2):
                off = h * 2 * ROWS if pair == 0 else (1 - h) * 2 * ROWS
                off = pl.multiple_of(off, 128)
                both = pl.ds(off, 2 * ROWS)
                val = jnp.dot(bb[pl.ds(pl.multiple_of(h * 2 * ROWS + off, 128), 2 * ROWS), :], cf[k, h, maj],
                              preferred_element_type=F32)
                er[k, h, maj, both, :] = (cb[k, h, maj, both, :].astype(F32) - val).astype(BF16)
                for mn in range(2):
                    if pair == 0:
                        send6(k, h, 2, maj, mn).start()
                        send6(k, h, 3, maj, mn).start()
                    else:
                        send6(k, h, 1, maj, mn).start()
                        keep6(k, h, maj, mn).start()
        halves(one)

    def send5_other(k, h):
        other = 1 - my_maj(k)
        return remote(cf.at[k, h, other], cf.at[k, h, other], s5.at[k, h], r5.at[k, h], p1(k, h))

    def ysend(k):
        return remote(ys.at[k], yr.at[k], ysm.at[k], yrm.at[k], at(yl_=1 - yl))

    def z_total(k):
        total = rep[k, z].astype(F32)
        for d in range(1, 8):
            zsend(k, d).wait_recv()
            total = total + rz[k, d].astype(F32)
        ys[k] = total
        ysend(k).start()

    def asend(k, d):
        return remote(mean.at[k, z], mean.at[k, z], as_.at[k, d], ar.at[k, d], at(z_=lax.rem(z + d, 8)))

    def arecv(k, d):
        frm = lax.rem(z - d + 8, 8)
        return remote(mean.at[k, frm], mean.at[k, frm], as_.at[k, d], ar.at[k, d], at(z_=lax.rem(z + d, 8)))

    def z_mean(k):
        ysend(k).wait_recv()
        mean[k, z] = ((ys[k] + yr[k]) * (1.0 / 16.0)).astype(BF16)
        for d in range(1, 8):
            asend(k, d).start()

    def outer(k):
        for d in range(1, 8):
            arecv(k, d).wait_recv()
        for h in range(2):
            lanes = pl.ds(h * 256 + k * LANES, LANES)
            og[:, lanes] = jnp.dot(bown[...], mean[k, :, h].reshape(RANK, LANES), preferred_element_type=F32)

    partial(0, 0)
    partial(1, 0)
    partial(0, 1)
    exchange(0)
    partial(1, 1)
    coefficients(0)
    rebuild(0, 0)
    exchange(1)
    z_total(0)
    coefficients(1)
    rebuild(1, 0)
    z_mean(0)
    rebuild(0, 1)
    z_total(1)

    @pl.when(off_diagonal)
    def _():
        own_rows.wait_recv()

    @pl.when(shard == replica)
    def _():
        own_rows_here.wait()

    outer(0)
    z_mean(1)
    rebuild(1, 1)
    outer(1)

    for cp in basis_sends:
        cp.wait_send()

    @pl.when(off_diagonal)
    def _():
        own_rows.wait_send()

    for k in range(STAGES):
        def one(h):
            for maj in range(2):
                for m in range(1, 4):
                    send1(k, h, m, maj).wait_send()
                    for mn in range(2):
                        send6(k, h, m, maj, mn).wait_send()
                        receive6(k, h, m, maj, mn).wait_recv()
                for mn in range(2):
                    keep6(k, h, maj, mn).wait()
            send2(k, h).wait_send()
            send3(k, h).wait_send()
            send5(k, h).wait_send()
        halves(one)
        for d in range(1, 8):
            zsend(k, d).wait_send()
            asend(k, d).wait_send()
        ysend(k).wait_send()


def exchange_step(grads, errors, basis):
    K = STAGES
    any_, vmem = pl.BlockSpec(memory_space=pl.ANY), pl.BlockSpec(memory_space=pltpu.VMEM)
    hbm = pl.BlockSpec(memory_space=pltpu.HBM)
    D = pltpu.SemaphoreType.DMA
    V = pltpu.VMEM
    return pl.pallas_call(
        kernel,
        out_shape=(jax.ShapeDtypeStruct(grads.shape, BF16), jax.ShapeDtypeStruct((ROWS, 512), F32)),
        in_specs=[hbm, hbm, hbm],
        out_specs=(any_, vmem),
        scratch_shapes=[
            V((K, 2, 4, 2, 2, ROWS, 256), BF16),
            V((K, 2, 3, 2, ROWS, 256), BF16),
            V((K, 2, 2, 4 * ROWS, 256), BF16),
            V((6 * ROWS, RANK), BF16),
            V((RANK, 6 * ROWS), BF16),
            V((K, 2, RANK, 256), BF16),
            V((K, 2, RANK, 256), F32),
            V((K, 2, RANK, 256), BF16),
            V((K, 2, RANK, 256), BF16),
            V((K, 2, RANK, 256), BF16),
            V((K, 2, 2, RANK, 256), BF16),
            V((K, 2, 2, 4 * ROWS, 256), BF16),
            V((K, 8, 2, 64, LANES), BF16),
            V((K, 8, 2, 64, LANES), BF16),
            V((K, 2, 64, LANES), F32),
            V((K, 2, 64, LANES), F32),
            V((K, 8, 2, 64, LANES), BF16),
            V((ROWS, RANK), BF16),
            D((K, 2, 4, 2)),
            D((6,)), D((6,)),
            D((K, 2, 3, 2)), D((K, 2, 3, 2)),
            D((K, 2)), D((K, 2)),
            D((K, 2)), D((K, 2)),
            D((K, 2)), D((K, 2)),
            D((K, 2, 3, 2, 2)), D((K, 2, 3, 2, 2)),
            D((K, 8)), D((K, 8)),
            D((K,)), D((K,)),
            D((K, 8)), D((K, 8)),
            D((K, 2, 2, 2)),
            D((2,)),
        ],
        compiler_params=pltpu.CompilerParams(
            collective_id=0, has_side_effects=True, vmem_limit_bytes=40 << 20),
        name="exchange_step",
    )(*(pltpu.with_memory_space_constraint(a, pltpu.HBM) for a in (grads, errors, basis)))


def body(grads, errors, basis, params, momentum):
    new_error, outer_grad = exchange_step(grads, errors, basis)
    new_momentum = momentum_rate * momentum + outer_grad
    new_params = params - outer_rate * (outer_grad + momentum_rate * new_momentum)
    return (new_params, new_momentum, new_error)


def solution(mesh):
    in_specs = (
        P("replica", "shard", None),
        P("replica", "shard", None),
        P("shard", None),
        P("replica", "shard"),
        P("replica", "shard"),
    )
    out_specs = (P("replica", "shard"), P("replica", "shard"), P("replica", "shard", None))
    return jax.shard_map(body, mesh=mesh, in_specs=in_specs, out_specs=out_specs, check_vma=False)
```

time: 201 us -> 88.2 us (0.44)
  the two profiles are of different devices: /device:TPU:1 before, /device:TPU:15 now
where the time goes in v1:
time: 88.2 us; the launch traced here: 88.1 us
  Pallas kernels  84.8 us (96%)
  local copies, waits for them, and re-layouts  1.67 us (2%)
  other arithmetic  1 us (1%)
    pallas_call x1, Pallas kernels, exchange_step(): pl.pallas_call(kernel, out_shape=(jax.ShapeDtypeStruct(grads.shape, BF16)...  84.8 us

profile of v1, /device:TPU:15, one launch (start us, length us, event | category | flops | bytes accessed | tf_op | source)
XLA Modules:
  0.0 88.1 jit_solution(15953741175260861899)
XLA Ops:
  0.6 0.0 copy-start.1
  0.6 0.0 copy-start
  0.7 84.8 %exchange_step.1 = (bf16[1,192,8192]{2,1,0:T(8,128)(2,1)S(1)}, f32[192,512]{1,0:T(8,128)S(1)}) custom-call(bf16[1,192,8192]{2,1,0:T(8,128)(2,1)} %g.1, bf16[1,192,8192]{2,1,0:T(8,128)(2,1)} %e.1, bf16[192,512]{1,0:T(8,128)(2,1)} %b.1), custom_call_target="tpu_custom_call" | custom-call | tf_op jit(solution)/shard_map/exchange_step/pallas_call | solution.py:360
  85.5 0.0 copy-done.1
  85.5 0.0 copy-done
  85.5 1.0 %multiply_subtract_fusion = (f32[192,512]{1,0:T(8,128)}, f32[192,512]{1,0:T(8,128)}) fusion(f32[192,512]{1,0:T(8,128)S(1)} %copy-done, f32[192,512]{1,0:T(8,128)S(1)} %get-tuple-element.5, f32[192,512]{1,0:T(8,128)S(1)} %copy-done.1), kind=kLoop, calls=%fused_computation | loop fusion | flops 589824 | bytes 1966080 | tf_op jit(solution)/shard_map/sub | solution.py:406
  86.5 1.7 %copy.9 = bf16[1,192,8192]{2,1,0:T(8,128)(2,1)} copy(bf16[1,192,8192]{2,1,0:T(8,128)(2,1)S(1)} %get-tuple-element.14) | data formatting | bytes 6291456
Async XLA Ops:
  0.6 84.8 %copy-start.1 = (f32[192,512]{1,0:T(8,128)S(1)}, f32[192,512]{1,0:T(8,128)}, u32[]{:S(2)}) copy-start(f32[192,512]{1,0:T(8,128)} %param.9) | copy-start | bytes 1179652
  0.6 84.8 %copy-start = (f32[192,512]{1,0:T(8,128)S(1)}, f32[192,512]{1,0:T(8,128)}, u32[]{:S(2)}) copy-start(f32[192,512]{1,0:T(8,128)} %param.8) | copy-start | bytes 1179652

commit v2 on v1

--- a/solution.py
+++ b/solution.py
@@ -13,9 +13,39 @@
 Y_FIRST = (True, True)
 STAGES = 2
 ROWS, RANK, LANES = 192, 512, 128
-
-
-def kernel(g, e, b, o, og, ge, sb, cb, bb, bt, ps, kp, pr, xs, xr, cf, er, rep, rz, ys, yr, mean, bown,
+SCHEDULE = (
+    ("basis_start",),
+    ("correct", 0, 0),
+    ("own_start",),
+    ("basis_pass", 0),
+    ("correct", 1, 0),
+    ("basis_pass", 1),
+    ("correct", 0, 1),
+    ("basis_pass", 2),
+    ("partial", 0, 0),
+    ("correct", 1, 1),
+    ("partial", 1, 0),
+    ("partial", 0, 1),
+    ("exchange", 0),
+    ("partial", 1, 1),
+    ("coefficients", 0),
+    ("rebuild", 0, 0),
+    ("exchange", 1),
+    ("z_total", 0),
+    ("coefficients", 1),
+    ("rebuild", 1, 0),
+    ("z_mean", 0),
+    ("rebuild", 0, 1),
+    ("z_total", 1),
+    ("own_wait",),
+    ("outer", 0),
+    ("z_mean", 1),
+    ("rebuild", 1, 1),
+    ("outer", 1),
+)
+
+
+def kernel(g, e, b, o, og, gb, eb, sb, cb, bb, bt, ps, kp, pr, xs, xr, cf, er, rep, rz, ys, yr, mean, bown,
            ldsem, bsem_s, bsem_r, s1, r1, s2, r2, s3, r3, s5, r5, s6, r6, zs, zr, ysm, yrm, as_, ar, osem, lsem):
     shard, replica = lax.axis_index("shard"), lax.axis_index("replica")
     yh, x, c = shard // 8, lax.rem(shard // 2, 4), lax.rem(shard, 2)
@@ -80,6 +110,15 @@
             return carry
         lax.fori_loop(0, 2, step, 0)
 
+    own_b = pltpu.make_async_copy(b, bb.at[pl.ds(2 * ROWS, ROWS)], lsem.at[0])
+    own_b.start()
+    loads = [
+        pltpu.make_async_copy(src.at[0, pl.ds(i * 96, 96)], dst.at[pl.ds(i * 96, 96)], ldsem.at[2 * w + i])
+        for i in range(2) for w, (src, dst) in enumerate(((g, gb), (e, eb)))
+    ]
+    for cp in loads:
+        cp.start()
+
     barrier = pltpu.get_barrier_semaphore()
     partners = [at(c_=1 - c), at(x_=na), at(x_=na, c_=1 - c), at(x_=nb), at(x_=nb, c_=1 - c), at(yh_=1 - yh),
                 at(yl_=1 - yl)] + [at(z_=lax.rem(z + d, 8)) for d in range(1, 8)]
@@ -91,98 +130,115 @@
     def _():
         pl.semaphore_signal(barrier, inc=1, device_id=(shard, replica), device_id_type=MESH)
 
-    own_b = pltpu.make_async_copy(b, bb.at[pl.ds(2 * ROWS, ROWS)], lsem.at[0])
-    own_b.start()
     order = (2, 3, 1, 0)
 
     def maj_of(k, m, s):
         return lax.rem(my_maj(k, m) + 1 + s, 2)
 
-    def load(k, s):
+    def correct(k, s):
         for m in order:
             def one(h):
                 maj = maj_of(k, m, s)
                 for mn in range(2):
                     cols = column(k, h, m, maj, mn)
-                    for w, src in enumerate((g, e)):
-                        pltpu.make_async_copy(
-                            src.at[0, :, cols], ge.at[k, h, m, maj, w, :, pl.ds(mn * LANES, LANES)],
-                            ldsem.at[k, h, m, maj]).start()
-            halves(one)
-
-    def correct(k, s):
-        for m in order:
-            def one(h):
-                maj = maj_of(k, m, s)
-                piece = ge.at[k, h, m, maj]
-                pltpu.make_async_copy(piece, piece, ldsem.at[k, h, m, maj]).wait()
-                val = (ge[k, h, m, maj, 0].astype(F32) + ge[k, h, m, maj, 1].astype(F32)).astype(BF16)
-                if m == 0:
-                    cb[k, h, maj, rows_of(h, 0), :] = val
-                else:
-                    sb[k, h, m - 1, maj] = val
+                    lanes = pl.ds(mn * LANES, LANES)
+                    val = (gb[:, cols].astype(F32) + eb[:, cols].astype(F32)).astype(BF16)
+                    if m == 0:
+                        cb[k, h, maj, rows_of(h, 0), lanes] = val
+                    else:
+                        sb[k, h, m - 1, maj, :, lanes] = val
+                if m:
                     send1(k, h, m, maj).start()
             halves(one)
 
     def send1(k, h, m, maj):
-        return remote(sb.at[k, h, m - 1, maj], cb.at[k, h, maj, rows_of(h, m)],
-                      s1.at[k, h, m - 1, maj], r1.at[k, h, m - 1, maj], member(h, m))
-
-    for k in range(STAGES):
-        for s in range(2):
-            load(k, s)
+        return remote(sb.at[k, h, m - 1, maj], cb.at[k, h, maj, rows_of(h, m)], s1.at[0], r1.at[k, h, maj], member(h, m))
+
+    def done(sem, like):
+        return pltpu.make_async_copy(like, like, sem)
 
     pl.semaphore_wait(barrier, len(partners) + jnp.where(off_diagonal, 1, 0))
 
     def slot(i):
         return bb.at[pl.ds(i * ROWS, ROWS)]
 
+    half = pl.ds(pl.multiple_of(lax.rem(z, 2) * 96, 96), 96)
+    rest = pl.ds(pl.multiple_of((1 - lax.rem(z, 2)) * 96, 96), 96)
+    zp = at(z_=z + 1 - 2 * lax.rem(z, 2))
+
+    def basis_copy(i, src, dst, dev):
+        return remote(src, dst, bsem_s.at[i], bsem_r.at[i], dev)
+
     own_b.wait()
-    basis_sends = [
-        remote(slot(2), slot(0), bsem_s.at[0], bsem_r.at[0], at(x_=na)),
-        remote(slot(2), slot(4), bsem_s.at[1], bsem_r.at[1], at(x_=nb)),
-        remote(slot(2), slot(3), bsem_s.at[2], bsem_r.at[2], at(c_=1 - c)),
-        remote(slot(0), slot(1), bsem_s.at[3], bsem_r.at[3], at(c_=1 - c)),
-        remote(slot(4), slot(5), bsem_s.at[4], bsem_r.at[4], at(c_=1 - c)),
-    ]
-    for cp in basis_sends[:3]:
-        cp.start()
-
-    correct(0, 0)
-    correct(1, 0)
-    for i in range(2):
-        basis_sends[i].wait_recv()
-        basis_sends[3 + i].start()
-    correct(0, 1)
-    correct(1, 1)
+    basis_copies = []
+    for i, (near, far, dev) in enumerate(((0, 1, at(x_=na)), (4, 5, at(x_=nb)))):
+        mine = slot(2).at[half]
+        basis_copies += [
+            basis_copy(6 * i, mine, slot(near).at[half], dev),
+            basis_copy(6 * i + 1, slot(near).at[half], slot(near).at[half], zp),
+            basis_copy(6 * i + 2, slot(near).at[half], slot(far).at[half], at(c_=1 - c)),
+            basis_copy(6 * i + 3, slot(near).at[rest], slot(far).at[rest], at(c_=1 - c)),
+        ]
+    basis_core = basis_copy(4, slot(2), slot(3), at(c_=1 - c))
+
+    def basis_from_z(i):
+        near = (0, 4)[i]
+        return basis_copy(6 * i + 1, slot(near).at[half], slot(near).at[rest], zp)
+
+    def basis_start():
+        basis_copies[0].start()
+        basis_copies[4].start()
+        basis_core.start()
+
+    def basis_pass(step):
+        for i in range(2):
+            if step == 0:
+                basis_copies[4 * i].wait_recv()
+                basis_copies[4 * i + 1].start()
+                basis_copies[4 * i + 2].start()
+            elif step == 1:
+                basis_from_z(i).wait_recv()
+                basis_copies[4 * i + 3].start()
+            else:
+                basis_copies[4 * i + 2].wait_recv()
+                basis_copies[4 * i + 3].wait_recv()
+        if step == 2:
+            basis_core.wait_recv()
+
+            def turn(i, carry):
+                at_ = pl.ds(pl.multiple_of(i * 2 * ROWS, 128), 2 * ROWS)
+                bt[:, at_] = bb[at_, :].T
+                return carry
+            lax.fori_loop(0, 3, turn, 0)
 
     own_rows = remote(slot(2), bown, bsem_s.at[5], bsem_r.at[5], (shard, replica))
     own_rows_here = pltpu.make_async_copy(slot(2), bown, lsem.at[1])
 
-    @pl.when(off_diagonal)
-    def _():
-        own_rows.start()
-
-    @pl.when(shard == replica)
-    def _():
-        own_rows_here.start()
-
-    for i in range(2, 5):
-        basis_sends[i].wait_recv()
-
-    def turn(i, carry):
-        bt[:, pl.ds(pl.multiple_of(i * 2 * ROWS, 128), 2 * ROWS)] = bb[pl.ds(pl.multiple_of(i * 2 * ROWS, 128), 2 * ROWS), :].T
-        return carry
-    lax.fori_loop(0, 3, turn, 0)
+    def own_start():
+        @pl.when(off_diagonal)
+        def _():
+            own_rows.start()
+
+        @pl.when(shard == replica)
+        def _():
+            own_rows_here.start()
+
+    def own_wait():
+        @pl.when(off_diagonal)
+        def _():
+            own_rows.wait_recv()
+
+        @pl.when(shard == replica)
+        def _():
+            own_rows_here.wait()
 
     def send2(k, h):
-        return remote(ps.at[k, h], pr.at[k, h], s2.at[k, h], r2.at[k, h], p1(k, h))
+        return remote(ps.at[k, h], pr.at[k, h], s2.at[0], r2.at[k, h], p1(k, h))
 
     def partial(k, s):
         def one(h):
             maj = maj_of(k, 0, s)
-            for m in range(1, 4):
-                send1(k, h, m, maj).wait_recv()
+            done(r1.at[k, h, maj], cb.at[k, h, maj, pl.ds(0, 3 * ROWS)]).wait()
 
             def tile(i, carry):
                 rk = pl.ds(pl.multiple_of(i * 256, 256), 256)
@@ -199,7 +255,7 @@
         halves(one)
 
     def send3(k, h):
-        return remote(xs.at[k, h], xr.at[k, h], s3.at[k, h], r3.at[k, h], p2(k, h))
+        return remote(xs.at[k, h], xr.at[k, h], s3.at[0], r3.at[k, h], p2(k, h))
 
     def exchange(k):
         def one(h):
@@ -209,11 +265,11 @@
         halves(one)
 
     def send5(k, h):
-        return remote(cf.at[k, h, my_maj(k)], cf.at[k, h, my_maj(k)], s5.at[k, h], r5.at[k, h], p1(k, h))
+        return remote(cf.at[k, h, my_maj(k)], cf.at[k, h, my_maj(k)], s5.at[0], r5.at[k, h], p1(k, h))
 
     def zsend(k, d):
         to = lax.rem(z + d, 8)
-        return remote(rep.at[k, to], rz.at[k, d], zs.at[k, d], zr.at[k, d], at(z_=to))
+        return remote(rep.at[k, to], rz.at[k, d], zs.at[0], zr.at[k], at(z_=to))
 
     def coefficients(k):
         def one(h):
@@ -229,16 +285,11 @@
     def send6(k, h, m, maj, mn):
         src = er.at[k, h, maj, rows_of(h, m), pl.ds(mn * LANES, LANES)]
         dst = o.at[0, :, column(k, h, 0, maj, mn)]
-        return remote(src, dst, s6.at[k, h, m - 1, maj, mn], r6.at[k, h, m - 1, maj, mn], member(h, m))
+        return remote(src, dst, s6.at[0], r6.at[0], member(h, m))
 
     def keep6(k, h, maj, mn):
         src = er.at[k, h, maj, rows_of(h, 0), pl.ds(mn * LANES, LANES)]
-        return pltpu.make_async_copy(src, o.at[0, :, column(k, h, 0, maj, mn)], osem.at[k, h, maj, mn])
-
-    def receive6(k, h, m, maj, mn):
-        src = er.at[k, h, maj, rows_of(h, m), pl.ds(mn * LANES, LANES)]
-        dst = o.at[0, :, column(k, h, m, maj, mn)]
-        return remote(src, dst, s6.at[k, h, m - 1, maj, mn], r6.at[k, h, m - 1, maj, mn], member(h, m))
+        return pltpu.make_async_copy(src, o.at[0, :, column(k, h, 0, maj, mn)], osem.at[0])
 
     def rebuild(k, s):
         def one(h):
@@ -263,25 +314,21 @@
 
     def send5_other(k, h):
         other = 1 - my_maj(k)
-        return remote(cf.at[k, h, other], cf.at[k, h, other], s5.at[k, h], r5.at[k, h], p1(k, h))
+        return remote(cf.at[k, h, other], cf.at[k, h, other], s5.at[0], r5.at[k, h], p1(k, h))
 
     def ysend(k):
         return remote(ys.at[k], yr.at[k], ysm.at[k], yrm.at[k], at(yl_=1 - yl))
 
     def z_total(k):
         total = rep[k, z].astype(F32)
+        done(zr.at[k], rz.at[k, pl.ds(1, 7)]).wait()
         for d in range(1, 8):
-            zsend(k, d).wait_recv()
             total = total + rz[k, d].astype(F32)
         ys[k] = total
         ysend(k).start()
 
     def asend(k, d):
-        return remote(mean.at[k, z], mean.at[k, z], as_.at[k, d], ar.at[k, d], at(z_=lax.rem(z + d, 8)))
-
-    def arecv(k, d):
-        frm = lax.rem(z - d + 8, 8)
-        return remote(mean.at[k, frm], mean.at[k, frm], as_.at[k, d], ar.at[k, d], at(z_=lax.rem(z + d, 8)))
+        return remote(mean.at[k, z], mean.at[k, z], as_.at[0], ar.at[k], at(z_=lax.rem(z + d, 8)))
 
     def z_mean(k):
         ysend(k).wait_recv()
@@ -290,65 +337,37 @@
             asend(k, d).start()
 
     def outer(k):
-        for d in range(1, 8):
-            arecv(k, d).wait_recv()
+        done(ar.at[k], rz.at[k, pl.ds(1, 7)]).wait()
         for h in range(2):
             lanes = pl.ds(h * 256 + k * LANES, LANES)
             og[:, lanes] = jnp.dot(bown[...], mean[k, :, h].reshape(RANK, LANES), preferred_element_type=F32)
 
-    partial(0, 0)
-    partial(1, 0)
-    partial(0, 1)
-    exchange(0)
-    partial(1, 1)
-    coefficients(0)
-    rebuild(0, 0)
-    exchange(1)
-    z_total(0)
-    coefficients(1)
-    rebuild(1, 0)
-    z_mean(0)
-    rebuild(0, 1)
-    z_total(1)
-
-    @pl.when(off_diagonal)
-    def _():
-        own_rows.wait_recv()
-
-    @pl.when(shard == replica)
-    def _():
-        own_rows_here.wait()
-
-    outer(0)
-    z_mean(1)
-    rebuild(1, 1)
-    outer(1)
-
-    for cp in basis_sends:
+    for cp in loads:
+        cp.wait()
+    events = dict(basis_start=basis_start, basis_pass=basis_pass, own_start=own_start, own_wait=own_wait, correct=correct,
+                  partial=partial, exchange=exchange, coefficients=coefficients, rebuild=rebuild, z_total=z_total,
+                  z_mean=z_mean, outer=outer)
+    for name, *where in SCHEDULE:
+        events[name](*where)
+
+    for cp in basis_copies + [basis_core]:
         cp.wait_send()
 
     @pl.when(off_diagonal)
     def _():
         own_rows.wait_send()
 
+    done(s1.at[0], sb).wait()
+    done(s2.at[0], ps).wait()
+    done(s3.at[0], xs).wait()
+    done(s5.at[0], pr).wait()
     for k in range(STAGES):
-        def one(h):
-            for maj in range(2):
-                for m in range(1, 4):
-                    send1(k, h, m, maj).wait_send()
-                    for mn in range(2):
-                        send6(k, h, m, maj, mn).wait_send()
-                        receive6(k, h, m, maj, mn).wait_recv()
-                for mn in range(2):
-                    keep6(k, h, maj, mn).wait()
-            send2(k, h).wait_send()
-            send3(k, h).wait_send()
-            send5(k, h).wait_send()
-        halves(one)
-        for d in range(1, 8):
-            zsend(k, d).wait_send()
-            asend(k, d).wait_send()
         ysend(k).wait_send()
+    done(zs.at[0], rz.at[:, pl.ds(1, 7)]).wait()
+    done(as_.at[0], rz.at[:, pl.ds(1, 7)]).wait()
+    done(osem.at[0], er.at[:, :, :, pl.ds(0, ROWS)]).wait()
+    done(s6.at[0], sb).wait()
+    done(r6.at[0], sb).wait()
 
 
 def exchange_step(grads, errors, basis):
@@ -363,7 +382,8 @@
         in_specs=[hbm, hbm, hbm],
         out_specs=(any_, vmem),
         scratch_shapes=[
-            V((K, 2, 4, 2, 2, ROWS, 256), BF16),
+            V((ROWS, 8192), BF16),
+            V((ROWS, 8192), BF16),
             V((K, 2, 3, 2, ROWS, 256), BF16),
             V((K, 2, 2, 4 * ROWS, 256), BF16),
             V((6 * ROWS, RANK), BF16),
@@ -381,17 +401,17 @@
             V((K, 2, 64, LANES), F32),
             V((K, 8, 2, 64, LANES), BF16),
             V((ROWS, RANK), BF16),
-            D((K, 2, 4, 2)),
-            D((6,)), D((6,)),
-            D((K, 2, 3, 2)), D((K, 2, 3, 2)),
-            D((K, 2)), D((K, 2)),
-            D((K, 2)), D((K, 2)),
-            D((K, 2)), D((K, 2)),
-            D((K, 2, 3, 2, 2)), D((K, 2, 3, 2, 2)),
-            D((K, 8)), D((K, 8)),
+            D((4,)),
+            D((10,)), D((10,)),
+            D((1,)), D((K, 2, 2)),
+            D((1,)), D((K, 2)),
+            D((1,)), D((K, 2)),
+            D((1,)), D((K, 2)),
+            D((1,)), D((1,)),
+            D((1,)), D((K,)),
             D((K,)), D((K,)),
-            D((K, 8)), D((K, 8)),
-            D((K, 2, 2, 2)),
+            D((1,)), D((K,)),
+            D((1,)),
             D((2,)),
         ],
         compiler_params=pltpu.CompilerParams(

time: 88.2 us -> 88.3 us (level)
  the two profiles are of different devices: /device:TPU:15 before, /device:TPU:1 now
where the time goes in v2:
time: 88.3 us; the launch traced here: 88.1 us
  Pallas kernels  84.8 us (96%)
  local copies, waits for them, and re-layouts  1.67 us (2%)
  other arithmetic  1 us (1%)
    pallas_call x1, Pallas kernels, exchange_step(): pl.pallas_call(kernel, out_shape=(jax.ShapeDtypeStruct(grads.shape, BF16)...  84.8 us

profile of v2, /device:TPU:1, one launch (start us, length us, event | category | flops | bytes accessed | tf_op | source)
XLA Modules:
  0.0 88.1 jit_solution(5730570740204698681)
XLA Ops:
  0.6 0.0 copy-start.1
  0.6 0.0 copy-start
  0.7 84.8 %exchange_step.1 = (bf16[1,192,8192]{2,1,0:T(8,128)(2,1)S(1)}, f32[192,512]{1,0:T(8,128)S(1)}) custom-call(bf16[1,192,8192]{2,1,0:T(8,128)(2,1)} %g.1, bf16[1,192,8192]{2,1,0:T(8,128)(2,1)} %e.1, bf16[192,512]{1,0:T(8,128)(2,1)} %b.1), custom_call_target="tpu_custom_call" | custom-call | tf_op jit(solution)/shard_map/exchange_step/pallas_call | solution.py:379
  85.4 0.0 copy-done.1
  85.4 0.0 copy-done
  85.5 1.0 %multiply_subtract_fusion = (f32[192,512]{1,0:T(8,128)}, f32[192,512]{1,0:T(8,128)}) fusion(f32[192,512]{1,0:T(8,128)S(1)} %copy-done, f32[192,512]{1,0:T(8,128)S(1)} %get-tuple-element.5, f32[192,512]{1,0:T(8,128)S(1)} %copy-done.1), kind=kLoop, calls=%fused_computation | loop fusion | flops 589824 | bytes 1966080 | tf_op jit(solution)/shard_map/sub | solution.py:426
  86.5 1.7 %copy.9 = bf16[1,192,8192]{2,1,0:T(8,128)(2,1)} copy(bf16[1,192,8192]{2,1,0:T(8,128)(2,1)S(1)} %get-tuple-element.14) | data formatting | bytes 6291456
Async XLA Ops:
  0.6 84.8 %copy-start.1 = (f32[192,512]{1,0:T(8,128)S(1)}, f32[192,512]{1,0:T(8,128)}, u32[]{:S(2)}) copy-start(f32[192,512]{1,0:T(8,128)} %param.9) | copy-start | bytes 1179652
  0.6 84.8 %copy-start = (f32[192,512]{1,0:T(8,128)S(1)}, f32[192,512]{1,0:T(8,128)}, u32[]{:S(2)}) copy-start(f32[192,512]{1,0:T(8,128)} %param.8) | copy-start | bytes 1179652

commit v3 on v2

v3 whole, which is shorter than its diff:
```python
import jax
import jax.numpy as jnp
from jax import lax
from jax.experimental import pallas as pl
from jax.experimental.pallas import tpu as pltpu
from jax.sharding import PartitionSpec as P

momentum_rate = 0.9
outer_rate = 0.7
MESH = pl.DeviceIdType.MESH
F32, BF16 = jnp.float32, jnp.bfloat16

STAGES = 2
ROWS, RANK, LANES = 192, 512, 128
SCHEDULE = (
    ("basis_start",),
    ("correct", 0, 0),
    ("correct", 1, 0),
    ("correct", 0, 1),
    ("correct", 1, 1),
    ("basis_pass", 0),
    ("basis_pass", 1),
    ("partial", 0, 0),
    ("basis_pass", 2),
    ("partial", 0, 1),
    ("partial", 1, 0),
    ("exchange", 0),
    ("partial", 1, 1),
    ("exchange", 1),
    ("own_start",),
    ("coefficients", 0, 0),
    ("coefficients", 1, 0),
    ("coefficients", 0, 1),
    ("coefficients", 1, 1),
    ("rebuild", 1, 0),
    ("z_total", 0, 0),
    ("rebuild", 0, 0),
    ("z_total", 1, 0),
    ("z_total", 0, 1),
    ("z_total", 1, 1),
    ("rebuild", 1, 1),
    ("z_mean", 0, 0),
    ("z_mean", 1, 0),
    ("z_mean", 0, 1),
    ("z_mean", 1, 1),
    ("rebuild", 0, 1),
    ("own_wait",),
    ("outer", 0, 0),
    ("outer", 1, 0),
    ("outer", 0, 1),
    ("outer", 1, 1),
)


def kernel(g, e, b, o, og, gb, eb, sb, cb, bb, bt, ps, kp, pr, xs, xr, cf, er, rep, rz, ys, yr, mean, bown,
           ldsem, bsem_s, bsem_r, s1, r1, s2, r2, s3, r3, s5, r5, s6, r6, zs, zr, ysm, yrm, as_, ar, osem, lsem):
    shard, replica = lax.axis_index("shard"), lax.axis_index("replica")
    yh, x, c = shard // 8, lax.rem(shard // 2, 4), lax.rem(shard, 2)
    yl, z = replica // 8, lax.rem(replica, 8)
    par = lax.rem(x, 2)
    na = x + 1 - 2 * par
    nb = lax.rem(x + 3 + 2 * par, 4)

    def at(yh_=None, x_=None, c_=None, yl_=None, z_=None):
        yh_ = yh if yh_ is None else yh_
        x_ = x if x_ is None else x_
        c_ = c if c_ is None else c_
        yl_ = yl if yl_ is None else yl_
        z_ = z if z_ is None else z_
        return (yl_ * 8 + z_, (yh_ * 4 + x_) * 2 + c_)

    def remote(src, dst, ss, rs, dev):
        return pltpu.make_async_remote_copy(
            src_ref=src, dst_ref=dst, send_sem=ss, recv_sem=rs, device_id=dev, device_id_type=MESH)

    def near(h):
        return na + h * (nb - na)

    def away(h):
        return nb + h * (na - nb)

    def member(k, h, m):
        c_m = c if m % 2 == 0 else 1 - c
        if m < 2:
            return at(c_=c_m)
        return at(x_=near(h), c_=c_m) if k == 0 else at(yh_=1 - yh, c_=c_m)

    def first_of(k, h, pair):
        if k == 1:
            return pair * 2 * ROWS
        return (h if pair == 0 else 1 - h) * 2 * ROWS

    def basis_row(k, h):
        return h * 2 * ROWS if k == 0 else 6 * ROWS

    def rows_of(k, h, m):
        row = first_of(k, h, 0 if m >= 2 else 1) + (m % 2) * ROWS
        return pl.ds(pl.multiple_of(row, ROWS), ROWS)

    def my_maj(k, h, m=0):
        if k == 0:
            return par if m < 2 else 1 - par
        odd = lax.rem((x + 1) // 2, 2)
        return odd + h * (x // 2 - odd)

    def my_min(k):
        return yh if k == 0 else par

    def column(k, h, m, maj, mn):
        c_d = c if m % 2 == 0 else 1 - c
        if k == 0:
            x_d = x if m < 2 else near(h)
            x_p = away(h) if m < 2 else lax.rem(x + 2, 4)
            y_o = mn
            x_o = x_d + (x_p - x_d) * lax.rem(lax.rem(x_d, 2) + maj, 2)
        else:
            y_o = yh if m < 2 else 1 - yh
            x_o = 2 * maj + mn * ((3 - 4 * maj) * (1 - h) + h)
        start = ((y_o * 4 + x_o) * 2 + c_d) * 512 + h * 256 + k * LANES
        return pl.ds(pl.multiple_of(start, LANES), LANES)

    def p1(k, h):
        return at(x_=away(h)) if k == 0 else at(x_=near(h))

    def p2(k, h):
        return at(yh_=1 - yh) if k == 0 else at(x_=away(h))

    def halves(body):
        def step(h, carry):
            body(h)
            return carry
        lax.fori_loop(0, 2, step, 0)

    def done(sem, like):
        return pltpu.make_async_copy(like, like, sem)

    own_b = pltpu.make_async_copy(b, bb.at[pl.ds(2 * ROWS, ROWS)], lsem.at[0])
    own_b.start()
    loads = [
        pltpu.make_async_copy(src.at[0, pl.ds(i * 96, 96)], dst.at[pl.ds(i * 96, 96)], ldsem.at[2 * w + i])
        for i in range(2) for w, (src, dst) in enumerate(((g, gb), (e, eb)))
    ]
    for cp in loads:
        cp.start()

    barrier = pltpu.get_barrier_semaphore()
    partners = [at(c_=1 - c), at(x_=na), at(x_=na, c_=1 - c), at(x_=nb), at(x_=nb, c_=1 - c), at(yh_=1 - yh),
                at(yh_=1 - yh, c_=1 - c), at(yl_=1 - yl)] + [at(z_=lax.rem(z + d, 8)) for d in range(1, 8)]
    for p in partners:
        pl.semaphore_signal(barrier, inc=1, device_id=p, device_id_type=MESH)
    off_diagonal = shard != replica

    @pl.when(off_diagonal)
    def _():
        pl.semaphore_signal(barrier, inc=1, device_id=(shard, replica), device_id_type=MESH)

    def maj_of(k, h, m, s):
        return lax.rem(my_maj(k, h, m) + 1 + s, 2)

    def send1(k, h, m, maj):
        return remote(sb.at[k, h, m - 1, maj], cb.at[k, h, maj, rows_of(k, h, m)], s1.at[0], r1.at[k, h, maj],
                      member(k, h, m))

    def correct(k, s):
        for m in (2, 3, 1, 0):
            def one(h):
                maj = maj_of(k, h, m, s)
                for mn in range(2):
                    cols = column(k, h, m, maj, mn)
                    lanes = pl.ds(mn * LANES, LANES)
                    val = (gb[:, cols].astype(F32) + eb[:, cols].astype(F32)).astype(BF16)
                    if m == 0:
                        cb[k, h, maj, rows_of(k, h, 0), lanes] = val
                    else:
                        sb[k, h, m - 1, maj, :, lanes] = val
                if m:
                    send1(k, h, m, maj).start()
            halves(one)

    pl.semaphore_wait(barrier, len(partners) + jnp.where(off_diagonal, 1, 0))

    def slot(i):
        return bb.at[pl.ds(i * ROWS, ROWS)]

    def basis_copy(i, src, dst, dev):
        return remote(slot(src), slot(dst), bsem_s.at[i], bsem_r.at[i], dev)

    core = at(c_=1 - c)
    own_b.wait()
    basis_out = [basis_copy(0, 2, 0, at(x_=na)), basis_copy(1, 2, 4, at(x_=nb)), basis_copy(2, 2, 6, at(yh_=1 - yh)),
                 basis_copy(3, 2, 3, core)]
    basis_on = [basis_copy(4, 0, 1, core), basis_copy(5, 4, 5, core), basis_copy(6, 6, 7, core)]

    def basis_start():
        for cp in basis_out:
            cp.start()

    def turn(first, last):
        def one(i, carry):
            at_ = pl.ds(pl.multiple_of(i * 2 * ROWS, 128), 2 * ROWS)
            bt[:, at_] = bb[at_, :].T
            return carry
        lax.fori_loop(first, last, one, 0)

    def basis_pass(step):
        if step == 0:
            for i in range(3):
                basis_out[i].wait_recv()
                basis_on[i].start()
        elif step == 1:
            basis_out[3].wait_recv()
            for i in range(2):
                basis_on[i].wait_recv()
            turn(0, 3)
        else:
            basis_on[2].wait_recv()
            bb[pl.ds(8 * ROWS, 2 * ROWS), :] = bb[pl.ds(2 * ROWS, 2 * ROWS), :]
            turn(3, 5)

    own_rows = remote(slot(2), bown, bsem_s.at[7], bsem_r.at[7], (shard, replica))
    own_rows_here = pltpu.make_async_copy(slot(2), bown, lsem.at[1])

    def own_start():
        @pl.when(off_diagonal)
        def _():
            own_rows.start()

        @pl.when(shard == replica)
        def _():
            own_rows_here.start()

    def own_wait():
        @pl.when(off_diagonal)
        def _():
            own_rows.wait_recv()

        @pl.when(shard == replica)
        def _():
            own_rows_here.wait()

    def send2(k, h):
        return remote(ps.at[k, h], pr.at[k, h], s2.at[0], r2.at[k, h], p1(k, h))

    def partial(k, s):
        def one(h):
            maj = maj_of(k, h, 0, s)
            done(r1.at[k, h, maj], cb.at[k, h, maj, pl.ds(0, 3 * ROWS)]).wait()

            def tile(i, carry):
                rk = pl.ds(pl.multiple_of(i * 256, 256), 256)
                val = jnp.dot(bt[rk, pl.ds(pl.multiple_of(basis_row(k, h), 128), 4 * ROWS)], cb[k, h, maj],
                              preferred_element_type=F32)
                if s == 0:
                    ps[k, h, rk, :] = val.astype(BF16)
                else:
                    kp[k, h, rk, :] = val
                return carry
            lax.fori_loop(0, 2, tile, 0)
            if s == 0:
                send2(k, h).start()
        halves(one)

    def send3(k, h):
        return remote(xs.at[k, h], xr.at[k, h], s3.at[0], r3.at[k, h], p2(k, h))

    def exchange(k):
        def one(h):
            send2(k, h).wait_recv()
            xs[k, h] = (kp[k, h] + pr[k, h].astype(F32)).astype(BF16)
            send3(k, h).start()
        halves(one)

    def send5(k, h, maj):
        return remote(cf.at[k, h, maj], cf.at[k, h, maj], s5.at[0], r5.at[k, h], p1(k, h))

    def zsend(k, h, d):
        to = lax.rem(z + d, 8)
        return remote(rep.at[k, h, to], rz.at[k, h, d], zs.at[0], zr.at[k, h], at(z_=to))

    def coefficients(k, h):
        maj = my_maj(k, h)
        send3(k, h).wait_recv()
        cf[k, h, maj] = (xs[k, h].astype(F32) + xr[k, h].astype(F32)).astype(BF16)
        mine = cf[k, h, maj, :, pl.ds(pl.multiple_of(my_min(k) * LANES, LANES), LANES)]
        rep[k, h] = mine.reshape(8, 64, LANES)
        send5(k, h, maj).start()
        for d in range(1, 8):
            zsend(k, h, d).start()

    def send6(k, h, m, maj, mn):
        src = er.at[k, h, maj, rows_of(k, h, m), pl.ds(mn * LANES, LANES)]
        return remote(src, o.at[0, :, column(k, h, 0, maj, mn)], s6.at[0], r6.at[0], member(k, h, m))

    def keep6(k, h, maj, mn):
        src = er.at[k, h, maj, rows_of(k, h, 0), pl.ds(mn * LANES, LANES)]
        return pltpu.make_async_copy(src, o.at[0, :, column(k, h, 0, maj, mn)], osem.at[0])

    def rebuild(k, s):
        def one(h):
            maj = lax.rem(my_maj(k, h) + s, 2)
            if s == 1:
                send5(k, h, maj).wait_recv()
            for pair in range(2):
                both = pl.ds(pl.multiple_of(first_of(k, h, pair), 128), 2 * ROWS)
                basis_rows = pl.ds(pl.multiple_of(basis_row(k, h) + first_of(k, h, pair), 128), 2 * ROWS)
                val = jnp.dot(bb[basis_rows, :], cf[k, h, maj], preferred_element_type=F32)
                er[k, h, maj, both, :] = (cb[k, h, maj, both, :].astype(F32) - val).astype(BF16)
                for mn in range(2):
                    if pair == 0:
                        send6(k, h, 2, maj, mn).start()
                        send6(k, h, 3, maj, mn).start()
                    else:
                        send6(k, h, 1, maj, mn).start()
                        keep6(k, h, maj, mn).start()
        halves(one)

    def ysend(k, h):
        return remote(ys.at[k, h], yr.at[k, h], ysm.at[k, h], yrm.at[k, h], at(yl_=1 - yl))

    def z_total(k, h):
        total = rep[k, h, z].astype(F32)
        done(zr.at[k, h], rz.at[k, h, pl.ds(1, 7)]).wait()
        for d in range(1, 8):
            total = total + rz[k, h, d].astype(F32)
        ys[k, h] = total
        ysend(k, h).start()

    def asend(k, h, d):
        return remote(mean.at[k, h, z], mean.at[k, h, z], as_.at[0], ar.at[k, h], at(z_=lax.rem(z + d, 8)))

    def z_mean(k, h):
        ysend(k, h).wait_recv()
        mean[k, h, z] = ((ys[k, h] + yr[k, h]) * (1.0 / 16.0)).astype(BF16)
        for d in range(1, 8):
            asend(k, h, d).start()

    def outer(k, h):
        done(ar.at[k, h], rz.at[k, h, pl.ds(1, 7)]).wait()
        og[:, pl.ds(h * 256 + k * LANES, LANES)] = jnp.dot(
            bown[...], mean[k, h].reshape(RANK, LANES), preferred_element_type=F32)

    for cp in loads:
        cp.wait()
    events = dict(basis_start=basis_start, basis_pass=basis_pass, own_start=own_start, own_wait=own_wait, correct=correct,
                  partial=partial, exchange=exchange, coefficients=coefficients, rebuild=rebuild, z_total=z_total,
                  z_mean=z_mean, outer=outer)
    for name, *where in SCHEDULE:
        events[name](*where)

    for cp in basis_out + basis_on:
        cp.wait_send()

    @pl.when(off_diagonal)
    def _():
        own_rows.wait_send()

    done(s1.at[0], sb).wait()
    done(s2.at[0], ps).wait()
    done(s3.at[0], xs).wait()
    done(s5.at[0], pr).wait()
    for k in range(STAGES):
        for h in range(2):
            ysend(k, h).wait_send()
    done(zs.at[0], rz.at[:, :, pl.ds(1, 7)]).wait()
    done(as_.at[0], rz.at[:, :, pl.ds(1, 7)]).wait()
    done(osem.at[0], er.at[:, :, :, pl.ds(0, ROWS)]).wait()
    done(s6.at[0], sb).wait()
    done(r6.at[0], sb).wait()


def exchange_step(grads, errors, basis):
    K = STAGES
    any_, vmem = pl.BlockSpec(memory_space=pl.ANY), pl.BlockSpec(memory_space=pltpu.VMEM)
    hbm = pl.BlockSpec(memory_space=pltpu.HBM)
    D = pltpu.SemaphoreType.DMA
    V = pltpu.VMEM
    return pl.pallas_call(
        kernel,
        out_shape=(jax.ShapeDtypeStruct(grads.shape, BF16), jax.ShapeDtypeStruct((ROWS, 512), F32)),
        in_specs=[hbm, hbm, hbm],
        out_specs=(any_, vmem),
        scratch_shapes=[
            V((ROWS, 8192), BF16),
            V((ROWS, 8192), BF16),
            V((K, 2, 3, 2, ROWS, 256), BF16),
            V((K, 2, 2, 4 * ROWS, 256), BF16),
            V((10 * ROWS, RANK), BF16),
            V((RANK, 10 * ROWS), BF16),
            V((K, 2, RANK, 256), BF16),
            V((K, 2, RANK, 256), F32),
            V((K, 2, RANK, 256), BF16),
            V((K, 2, RANK, 256), BF16),
            V((K, 2, RANK, 256), BF16),
            V((K, 2, 2, RANK, 256), BF16),
            V((K, 2, 2, 4 * ROWS, 256), BF16),
            V((K, 2, 8, 64, LANES), BF16),
            V((K, 2, 8, 64, LANES), BF16),
            V((K, 2, 64, LANES), F32),
            V((K, 2, 64, LANES), F32),
            V((K, 2, 8, 64, LANES), BF16),
            V((ROWS, RANK), BF16),
            D((4,)),
            D((8,)), D((8,)),
            D((1,)), D((K, 2, 2)),
            D((1,)), D((K, 2)),
            D((1,)), D((K, 2)),
            D((1,)), D((K, 2)),
            D((1,)), D((1,)),
            D((1,)), D((K, 2)),
            D((K, 2)), D((K, 2)),
            D((1,)), D((K, 2)),
            D((1,)),
            D((2,)),
        ],
        compiler_params=pltpu.CompilerParams(
            collective_id=0, has_side_effects=True, vmem_limit_bytes=40 << 20),
        name="exchange_step",
    )(*(pltpu.with_memory_space_constraint(a, pltpu.HBM) for a in (grads, errors, basis)))


def body(grads, errors, basis, params, momentum):
    new_error, outer_grad = exchange_step(grads, errors, basis)
    new_momentum = momentum_rate * momentum + outer_grad
    new_params = params - outer_rate * (outer_grad + momentum_rate * new_momentum)
    return (new_params, new_momentum, new_error)


def solution(mesh):
    in_specs = (
        P("replica", "shard", None),
        P("replica", "shard", None),
        P("shard", None),
        P("replica", "shard"),
        P("replica", "shard"),
    )
    out_specs = (P("replica", "shard"), P("replica", "shard"), P("replica", "shard", None))
    return jax.shard_map(body, mesh=mesh, in_specs=in_specs, out_specs=out_specs, check_vma=False)
```

time: 88.3 us -> 84.2 us (0.954)
  the two profiles are of different devices: /device:TPU:1 before, /device:TPU:10 now
where the time goes in v3:
time: 84.2 us
  Pallas kernels  80.8 us (96%)
  local copies, waits for them, and re-layouts  1.67 us (2%)
  other arithmetic  1 us (1%)
    pallas_call x1, Pallas kernels, exchange_step(): pl.pallas_call(kernel, out_shape=(jax.ShapeDtypeStruct(grads.shape, BF16)...  80.8 us

profile of v3, /device:TPU:10, one launch (start us, length us, event | category | flops | bytes accessed | tf_op | source)
XLA Modules:
  0.0 84.2 jit_solution(15443080630631073423)
XLA Ops:
  0.6 0.0 copy-start.1
  0.6 0.0 copy-start
  0.7 80.8 %exchange_step.1 = (bf16[1,192,8192]{2,1,0:T(8,128)(2,1)S(1)}, f32[192,512]{1,0:T(8,128)S(1)}) custom-call(bf16[1,192,8192]{2,1,0:T(8,128)(2,1)} %g.1, bf16[1,192,8192]{2,1,0:T(8,128)(2,1)} %e.1, bf16[192,512]{1,0:T(8,128)(2,1)} %b.1), custom_call_target="tpu_custom_call" | custom-call | tf_op jit(solution)/shard_map/exchange_step/pallas_call | solution.py:377
  81.5 0.0 copy-done.1
  81.5 0.0 copy-done
  81.5 1.0 %multiply_subtract_fusion = (f32[192,512]{1,0:T(8,128)}, f32[192,512]{1,0:T(8,128)}) fusion(f32[192,512]{1,0:T(8,128)S(1)} %copy-done, f32[192,512]{1,0:T(8,128)S(1)} %get-tuple-element.5, f32[192,512]{1,0:T(8,128)S(1)} %copy-done.1), kind=kLoop, calls=%fused_computation | loop fusion | flops 589824 | bytes 1966080 | tf_op jit(solution)/shard_map/sub | solution.py:424
  82.5 1.7 %copy.9 = bf16[1,192,8192]{2,1,0:T(8,128)(2,1)} copy(bf16[1,192,8192]{2,1,0:T(8,128)(2,1)S(1)} %get-tuple-element.14) | data formatting | bytes 6291456
Async XLA Ops:
  0.6 80.9 %copy-start.1 = (f32[192,512]{1,0:T(8,128)S(1)}, f32[192,512]{1,0:T(8,128)}, u32[]{:S(2)}) copy-start(f32[192,512]{1,0:T(8,128)} %param.9) | copy-start | bytes 1179652
  0.6 80.9 %copy-start = (f32[192,512]{1,0:T(8,128)S(1)}, f32[192,512]{1,0:T(8,128)}, u32[]{:S(2)}) copy-start(f32[192,512]{1,0:T(8,128)} %param.8) | copy-start | bytes 1179652

commit v4 on v3

--- a/solution.py
+++ b/solution.py
@@ -24,35 +24,40 @@
     ("basis_pass", 2),
     ("partial", 0, 1),
     ("partial", 1, 0),
+    ("own_start",),
     ("exchange", 0),
     ("partial", 1, 1),
     ("exchange", 1),
-    ("own_start",),
+    ("own_relay",),
     ("coefficients", 0, 0),
     ("coefficients", 1, 0),
+    ("coefficients", 1, 1),
+    ("rebuild", 1, 0, 0),
     ("coefficients", 0, 1),
-    ("coefficients", 1, 1),
-    ("rebuild", 1, 0),
     ("z_total", 0, 0),
-    ("rebuild", 0, 0),
+    ("rebuild", 1, 0, 1),
     ("z_total", 1, 0),
+    ("rebuild", 0, 0, 0),
+    ("z_total", 1, 1),
+    ("z_mean", 0, 0),
+    ("rebuild", 0, 0, 1),
+    ("rebuild", 1, 1, 0),
     ("z_total", 0, 1),
-    ("z_total", 1, 1),
-    ("rebuild", 1, 1),
-    ("z_mean", 0, 0),
     ("z_mean", 1, 0),
+    ("rebuild", 1, 1, 1),
+    ("z_mean", 1, 1),
+    ("rebuild", 0, 1, 0),
     ("z_mean", 0, 1),
-    ("z_mean", 1, 1),
-    ("rebuild", 0, 1),
+    ("rebuild", 0, 1, 1),
     ("own_wait",),
     ("outer", 0, 0),
     ("outer", 1, 0),
+    ("outer", 1, 1),
     ("outer", 0, 1),
-    ("outer", 1, 1),
 )
 
 
-def kernel(g, e, b, o, og, gb, eb, sb, cb, bb, bt, ps, kp, pr, xs, xr, cf, er, rep, rz, ys, yr, mean, bown,
+def kernel(g, e, b, o, og, gb, eb, sb, cb, bb, bt, ps, kp, pr, xs, xr, cf, er, rep, rz, ys, yr, mean,
            ldsem, bsem_s, bsem_r, s1, r1, s2, r2, s3, r3, s5, r5, s6, r6, zs, zr, ysm, yrm, as_, ar, osem, lsem):
     shard, replica = lax.axis_index("shard"), lax.axis_index("replica")
     yh, x, c = shard // 8, lax.rem(shard // 2, 4), lax.rem(shard, 2)
@@ -148,12 +153,6 @@
                 at(yh_=1 - yh, c_=1 - c), at(yl_=1 - yl)] + [at(z_=lax.rem(z + d, 8)) for d in range(1, 8)]
     for p in partners:
         pl.semaphore_signal(barrier, inc=1, device_id=p, device_id_type=MESH)
-    off_diagonal = shard != replica
-
-    @pl.when(off_diagonal)
-    def _():
-        pl.semaphore_signal(barrier, inc=1, device_id=(shard, replica), device_id_type=MESH)
-
     def maj_of(k, h, m, s):
         return lax.rem(my_maj(k, h, m) + 1 + s, 2)
 
@@ -177,7 +176,7 @@
                     send1(k, h, m, maj).start()
             halves(one)
 
-    pl.semaphore_wait(barrier, len(partners) + jnp.where(off_diagonal, 1, 0))
+    pl.semaphore_wait(barrier, len(partners))
 
     def slot(i):
         return bb.at[pl.ds(i * ROWS, ROWS)]
@@ -217,26 +216,60 @@
             bb[pl.ds(8 * ROWS, 2 * ROWS), :] = bb[pl.ds(2 * ROWS, 2 * ROWS), :]
             turn(3, 5)
 
-    own_rows = remote(slot(2), bown, bsem_s.at[7], bsem_r.at[7], (shard, replica))
-    own_rows_here = pltpu.make_async_copy(slot(2), bown, lsem.at[1])
+    side = lax.rem(z // 2 - x + 4, 4)
+    other = lax.rem(lax.rem(z, 2) + c, 2)
+    level = lax.rem(yh + yl, 2)
+    near_slot = jnp.where(side == 0, 2, jnp.where(side == 1, 4 * par, 4 - 4 * par)) + other
+    far = jnp.logical_or(jnp.logical_and(level == 0, side == 2), jnp.logical_and(level == 1, side != 0))
+    own_slot = jnp.where(far, 10, jnp.where(level == 0, near_slot, 6 + other))
+    to_right = jnp.logical_or(jnp.logical_and(level == 0, side == 3), jnp.logical_and(level == 1, side == 0))
+    to_left = jnp.logical_and(level == 1, side == 0)
+    on_right = jnp.logical_and(level == 1, side == 3)
+    right, left = at(x_=lax.rem(x + 1, 4)), at(x_=lax.rem(x + 3, 4))
+
+    def part(row, half):
+        return bb.at[pl.ds(pl.multiple_of(row * ROWS + half * 96, 96), 96)]
+
+    own_right = remote(part(own_slot, c), part(10, c), bsem_s.at[7], bsem_r.at[7], right)
+    own_left = remote(part(own_slot, c), part(10, c), bsem_s.at[8], bsem_r.at[7], left)
+    own_core = remote(part(10, c), part(10, c), bsem_s.at[9], bsem_r.at[8], core)
 
     def own_start():
-        @pl.when(off_diagonal)
-        def _():
-            own_rows.start()
-
-        @pl.when(shard == replica)
-        def _():
-            own_rows_here.start()
+        @pl.when(to_right)
+        def _():
+            own_right.start()
+
+        @pl.when(to_left)
+        def _():
+            own_left.start()
+
+    def own_relay():
+        @pl.when(far)
+        def _():
+            own_right.wait_recv()
+            own_core.start()
+
+        @pl.when(on_right)
+        def _():
+            own_right.start()
 
     def own_wait():
-        @pl.when(off_diagonal)
-        def _():
-            own_rows.wait_recv()
-
-        @pl.when(shard == replica)
-        def _():
-            own_rows_here.wait()
+        @pl.when(far)
+        def _():
+            own_core.wait_recv()
+
+    def own_end():
+        @pl.when(jnp.logical_or(to_right, on_right))
+        def _():
+            own_right.wait_send()
+
+        @pl.when(to_left)
+        def _():
+            own_left.wait_send()
+
+        @pl.when(far)
+        def _():
+            own_core.wait_send()
 
     def send2(k, h):
         return remote(ps.at[k, h], pr.at[k, h], s2.at[0], r2.at[k, h], p1(k, h))
@@ -295,24 +328,22 @@
         src = er.at[k, h, maj, rows_of(k, h, 0), pl.ds(mn * LANES, LANES)]
         return pltpu.make_async_copy(src, o.at[0, :, column(k, h, 0, maj, mn)], osem.at[0])
 
-    def rebuild(k, s):
-        def one(h):
-            maj = lax.rem(my_maj(k, h) + s, 2)
-            if s == 1:
-                send5(k, h, maj).wait_recv()
-            for pair in range(2):
-                both = pl.ds(pl.multiple_of(first_of(k, h, pair), 128), 2 * ROWS)
-                basis_rows = pl.ds(pl.multiple_of(basis_row(k, h) + first_of(k, h, pair), 128), 2 * ROWS)
-                val = jnp.dot(bb[basis_rows, :], cf[k, h, maj], preferred_element_type=F32)
-                er[k, h, maj, both, :] = (cb[k, h, maj, both, :].astype(F32) - val).astype(BF16)
-                for mn in range(2):
-                    if pair == 0:
-                        send6(k, h, 2, maj, mn).start()
-                        send6(k, h, 3, maj, mn).start()
-                    else:
-                        send6(k, h, 1, maj, mn).start()
-                        keep6(k, h, maj, mn).start()
-        halves(one)
+    def rebuild(k, s, h):
+        maj = lax.rem(my_maj(k, h) + s, 2)
+        if s == 1:
+            send5(k, h, maj).wait_recv()
+        for pair in range(2):
+            both = pl.ds(pl.multiple_of(first_of(k, h, pair), 128), 2 * ROWS)
+            basis_rows = pl.ds(pl.multiple_of(basis_row(k, h) + first_of(k, h, pair), 128), 2 * ROWS)
+            val = jnp.dot(bb[basis_rows, :], cf[k, h, maj], preferred_element_type=F32)
+            er[k, h, maj, both, :] = (cb[k, h, maj, both, :].astype(F32) - val).astype(BF16)
+            for mn in range(2):
+                if pair == 0:
+                    send6(k, h, 2, maj, mn).start()
+                    send6(k, h, 3, maj, mn).start()
+                else:
+                    send6(k, h, 1, maj, mn).start()
+                    keep6(k, h, maj, mn).start()
 
     def ysend(k, h):
         return remote(ys.at[k, h], yr.at[k, h], ysm.at[k, h], yrm.at[k, h], at(yl_=1 - yl))
@@ -337,11 +368,11 @@
     def outer(k, h):
         done(ar.at[k, h], rz.at[k, h, pl.ds(1, 7)]).wait()
         og[:, pl.ds(h * 256 + k * LANES, LANES)] = jnp.dot(
-            bown[...], mean[k, h].reshape(RANK, LANES), preferred_element_type=F32)
+            bb[pl.ds(pl.multiple_of(own_slot * ROWS, ROWS), ROWS), :], mean[k, h].reshape(RANK, LANES), preferred_element_type=F32)
 
     for cp in loads:
         cp.wait()
-    events = dict(basis_start=basis_start, basis_pass=basis_pass, own_start=own_start, own_wait=own_wait, correct=correct,
+    events = dict(basis_start=basis_start, basis_pass=basis_pass, own_start=own_start, own_relay=own_relay, own_wait=own_wait, correct=correct,
                   partial=partial, exchange=exchange, coefficients=coefficients, rebuild=rebuild, z_total=z_total,
                   z_mean=z_mean, outer=outer)
     for name, *where in SCHEDULE:
@@ -350,9 +381,7 @@
     for cp in basis_out + basis_on:
         cp.wait_send()
 
-    @pl.when(off_diagonal)
-    def _():
-        own_rows.wait_send()
+    own_end()
 
     done(s1.at[0], sb).wait()
     done(s2.at[0], ps).wait()
@@ -384,7 +413,7 @@
             V((ROWS, 8192), BF16),
             V((K, 2, 3, 2, ROWS, 256), BF16),
             V((K, 2, 2, 4 * ROWS, 256), BF16),
-            V((10 * ROWS, RANK), BF16),
+            V((11 * ROWS, RANK), BF16),
             V((RANK, 10 * ROWS), BF16),
             V((K, 2, RANK, 256), BF16),
             V((K, 2, RANK, 256), F32),
@@ -398,9 +427,8 @@
             V((K, 2, 64, LANES), F32),
             V((K, 2, 64, LANES), F32),
             V((K, 2, 8, 64, LANES), BF16),
-            V((ROWS, RANK), BF16),
             D((4,)),
-            D((8,)), D((8,)),
+            D((10,)), D((9,)),
             D((1,)), D((K, 2, 2)),
             D((1,)), D((K, 2)),
             D((1,)), D((K, 2)),
@@ -410,7 +438,7 @@
             D((K, 2)), D((K, 2)),
             D((1,)), D((K, 2)),
             D((1,)),
-            D((2,)),
+            D((1,)),
         ],
         compiler_params=pltpu.CompilerParams(
             collective_id=0, has_side_effects=True, vmem_limit_bytes=40 << 20),

time: 84.2 us -> 74.6 us (0.89)
  the two profiles are of different devices: /device:TPU:10 before, /device:TPU:1 now
where the time goes in v4:
time: 74.6 us; the launch traced here: 74.5 us
  Pallas kernels  71.1 us (95%)
  local copies, waits for them, and re-layouts  1.67 us (2%)
  other arithmetic  1 us (1%)
    pallas_call x1, Pallas kernels, exchange_step(): pl.pallas_call(kernel, out_shape=(jax.ShapeDtypeStruct(grads.shape, BF16)...  71.1 us
    unnamed x5, local copies, waits for them, and re-layouts  1.67 us

profile of v4, /device:TPU:1, one launch (start us, length us, event | category | flops | bytes accessed | tf_op | source)
XLA Modules:
  0.0 74.5 jit_solution(11306733381222290722)
XLA Ops:
  0.6 0.0 copy-start.1
  0.6 0.0 copy-start
  0.7 71.1 %exchange_step.1 = (bf16[1,192,8192]{2,1,0:T(8,128)(2,1)S(1)}, f32[192,512]{1,0:T(8,128)S(1)}) custom-call(bf16[1,192,8192]{2,1,0:T(8,128)(2,1)} %g.1, bf16[1,192,8192]{2,1,0:T(8,128)(2,1)} %e.1, bf16[192,512]{1,0:T(8,128)(2,1)} %b.1), custom_call_target="tpu_custom_call" | custom-call | tf_op jit(solution)/shard_map/exchange_step/pallas_call | solution.py:406
  71.8 0.0 copy-done.1
  71.8 0.0 copy-done
  71.8 1.0 %multiply_subtract_fusion = (f32[192,512]{1,0:T(8,128)}, f32[192,512]{1,0:T(8,128)}) fusion(f32[192,512]{1,0:T(8,128)S(1)} %copy-done, f32[192,512]{1,0:T(8,128)S(1)} %get-tuple-element.5, f32[192,512]{1,0:T(8,128)S(1)} %copy-done.1), kind=kLoop, calls=%fused_computation | loop fusion | flops 589824 | bytes 1966080 | tf_op jit(solution)/shard_map/sub | solution.py:452
  72.8 1.7 %copy.9 = bf16[1,192,8192]{2,1,0:T(8,128)(2,1)} copy(bf16[1,192,8192]{2,1,0:T(8,128)(2,1)S(1)} %get-tuple-element.14) | data formatting | bytes 6291456
Async XLA Ops:
  0.6 71.2 %copy-start.1 = (f32[192,512]{1,0:T(8,128)S(1)}, f32[192,512]{1,0:T(8,128)}, u32[]{:S(2)}) copy-start(f32[192,512]{1,0:T(8,128)} %param.9) | copy-start | bytes 1179652
  0.6 71.2 %copy-start = (f32[192,512]{1,0:T(8,128)S(1)}, f32[192,512]{1,0:T(8,128)}, u32[]{:S(2)}) copy-start(f32[192,512]{1,0:T(8,128)} %param.8) | copy-start | bytes 1179652

commit v5 on v4

--- a/solution.py
+++ b/solution.py
@@ -16,9 +16,9 @@
     ("basis_start",),
     ("correct", 0, 0),
     ("correct", 1, 0),
+    ("basis_pass", 0),
     ("correct", 0, 1),
     ("correct", 1, 1),
-    ("basis_pass", 0),
     ("basis_pass", 1),
     ("partial", 0, 0),
     ("basis_pass", 2),
@@ -30,24 +30,24 @@
     ("exchange", 1),
     ("own_relay",),
     ("coefficients", 0, 0),
+    ("rebuild", 0, 0, 0),
     ("coefficients", 1, 0),
     ("coefficients", 1, 1),
+    ("coefficients", 0, 1),
     ("rebuild", 1, 0, 0),
-    ("coefficients", 0, 1),
     ("z_total", 0, 0),
     ("rebuild", 1, 0, 1),
+    ("rebuild", 0, 0, 1),
     ("z_total", 1, 0),
-    ("rebuild", 0, 0, 0),
     ("z_total", 1, 1),
     ("z_mean", 0, 0),
-    ("rebuild", 0, 0, 1),
+    ("z_total", 0, 1),
     ("rebuild", 1, 1, 0),
-    ("z_total", 0, 1),
     ("z_mean", 1, 0),
+    ("z_mean", 1, 1),
     ("rebuild", 1, 1, 1),
-    ("z_mean", 1, 1),
+    ("z_mean", 0, 1),
     ("rebuild", 0, 1, 0),
-    ("z_mean", 0, 1),
     ("rebuild", 0, 1, 1),
     ("own_wait",),
     ("outer", 0, 0),
@@ -181,18 +181,32 @@
     def slot(i):
         return bb.at[pl.ds(i * ROWS, ROWS)]
 
+    odd_z = lax.rem(z, 2)
+    z_one, z_two = at(z_=z + 1 - 2 * odd_z), at(z_=lax.rem(z + 7 + 2 * odd_z, 8))
+
+    def half(i, which):
+        return bb.at[pl.ds(pl.multiple_of(i * ROWS + which * 96, 96), 96)]
+
     def basis_copy(i, src, dst, dev):
-        return remote(slot(src), slot(dst), bsem_s.at[i], bsem_r.at[i], dev)
+        return remote(src, dst, bsem_s.at[i], bsem_r.at[i], dev)
 
     core = at(c_=1 - c)
     own_b.wait()
-    basis_out = [basis_copy(0, 2, 0, at(x_=na)), basis_copy(1, 2, 4, at(x_=nb)), basis_copy(2, 2, 6, at(yh_=1 - yh)),
-                 basis_copy(3, 2, 3, core)]
-    basis_on = [basis_copy(4, 0, 1, core), basis_copy(5, 4, 5, core), basis_copy(6, 6, 7, core)]
+    basis_out, basis_z, basis_z_in, basis_on, basis_on_z = [], [], [], [], []
+    for i, (n, dev, zdev) in enumerate(((0, at(x_=na), z_one), (4, at(x_=nb), z_two), (6, at(yh_=1 - yh), z_one))):
+        basis_out.append(basis_copy(4 * i, half(2, odd_z), half(n, odd_z), dev))
+        basis_z.append(basis_copy(4 * i + 1, half(n, odd_z), half(n, odd_z), zdev))
+        basis_z_in.append(basis_copy(4 * i + 1, half(n, 1 - odd_z), half(n, 1 - odd_z), zdev))
+        basis_on.append(basis_copy(4 * i + 2, half(n, odd_z), half(n + 1, odd_z), core))
+        basis_on_z.append(basis_copy(4 * i + 3, half(n, 1 - odd_z), half(n + 1, 1 - odd_z), core))
+    basis_core = basis_copy(12, slot(2), slot(3), core)
 
     def basis_start():
         for cp in basis_out:
             cp.start()
+        basis_core.start()
+        for cp in loads:
+            cp.wait()
 
     def turn(first, last):
         def one(i, carry):
@@ -205,16 +219,22 @@
         if step == 0:
             for i in range(3):
                 basis_out[i].wait_recv()
+                basis_z[i].start()
                 basis_on[i].start()
-        elif step == 1:
-            basis_out[3].wait_recv()
-            for i in range(2):
+        else:
+            for i in range(2) if step == 1 else (2,):
+                basis_z_in[i].wait_recv()
+                basis_on_z[i].start()
+            if step == 1:
+                basis_core.wait_recv()
+            for i in range(2) if step == 1 else (2,):
                 basis_on[i].wait_recv()
-            turn(0, 3)
-        else:
-            basis_on[2].wait_recv()
-            bb[pl.ds(8 * ROWS, 2 * ROWS), :] = bb[pl.ds(2 * ROWS, 2 * ROWS), :]
-            turn(3, 5)
+                basis_on_z[i].wait_recv()
+            if step == 1:
+                turn(0, 3)
+            else:
+                bb[pl.ds(8 * ROWS, 2 * ROWS), :] = bb[pl.ds(2 * ROWS, 2 * ROWS), :]
+                turn(3, 5)
 
     side = lax.rem(z // 2 - x + 4, 4)
     other = lax.rem(lax.rem(z, 2) + c, 2)
@@ -230,9 +250,9 @@
     def part(row, half):
         return bb.at[pl.ds(pl.multiple_of(row * ROWS + half * 96, 96), 96)]
 
-    own_right = remote(part(own_slot, c), part(10, c), bsem_s.at[7], bsem_r.at[7], right)
-    own_left = remote(part(own_slot, c), part(10, c), bsem_s.at[8], bsem_r.at[7], left)
-    own_core = remote(part(10, c), part(10, c), bsem_s.at[9], bsem_r.at[8], core)
+    own_right = remote(part(own_slot, c), part(10, c), bsem_s.at[13], bsem_r.at[13], right)
+    own_left = remote(part(own_slot, c), part(10, c), bsem_s.at[14], bsem_r.at[13], left)
+    own_core = remote(part(10, c), part(10, c), bsem_s.at[15], bsem_r.at[14], core)
 
     def own_start():
         @pl.when(to_right)
@@ -316,9 +336,9 @@
         cf[k, h, maj] = (xs[k, h].astype(F32) + xr[k, h].astype(F32)).astype(BF16)
         mine = cf[k, h, maj, :, pl.ds(pl.multiple_of(my_min(k) * LANES, LANES), LANES)]
         rep[k, h] = mine.reshape(8, 64, LANES)
-        send5(k, h, maj).start()
         for d in range(1, 8):
             zsend(k, h, d).start()
+        send5(k, h, maj).start()
 
     def send6(k, h, m, maj, mn):
         src = er.at[k, h, maj, rows_of(k, h, m), pl.ds(mn * LANES, LANES)]
@@ -370,15 +390,13 @@
         og[:, pl.ds(h * 256 + k * LANES, LANES)] = jnp.dot(
             bb[pl.ds(pl.multiple_of(own_slot * ROWS, ROWS), ROWS), :], mean[k, h].reshape(RANK, LANES), preferred_element_type=F32)
 
-    for cp in loads:
-        cp.wait()
     events = dict(basis_start=basis_start, basis_pass=basis_pass, own_start=own_start, own_relay=own_relay, own_wait=own_wait, correct=correct,
                   partial=partial, exchange=exchange, coefficients=coefficients, rebuild=rebuild, z_total=z_total,
                   z_mean=z_mean, outer=outer)
     for name, *where in SCHEDULE:
         events[name](*where)
 
-    for cp in basis_out + basis_on:
+    for cp in basis_out + basis_z + basis_on + basis_on_z + [basis_core]:
         cp.wait_send()
 
     own_end()
@@ -428,7 +446,7 @@
             V((K, 2, 64, LANES), F32),
             V((K, 2, 8, 64, LANES), BF16),
             D((4,)),
-            D((10,)), D((9,)),
+            D((16,)), D((15,)),
             D((1,)), D((K, 2, 2)),
             D((1,)), D((K, 2)),
             D((1,)), D((K, 2)),

time: 74.6 us -> 75 us (level)
  no operation moved by 1% of the time
where the time goes in v5:
time: 75 us; the launch traced here: 74.9 us
  Pallas kernels  71.6 us (95%)
  local copies, waits for them, and re-layouts  1.67 us (2%)
  other arithmetic  1 us (1%)
    pallas_call x1, Pallas kernels, exchange_step(): pl.pallas_call(kernel, out_shape=(jax.ShapeDtypeStruct(grads.shape, BF16)...  71.6 us
    unnamed x5, local copies, waits for them, and re-layouts  1.67 us

profile of v5, /device:TPU:1, one launch (start us, length us, event | category | flops | bytes accessed | tf_op | source)
XLA Modules:
  0.0 74.9 jit_solution(42878512453167310)
XLA Ops:
  0.6 0.0 copy-start.1
  0.6 0.0 copy-start
  0.7 71.6 %exchange_step.1 = (bf16[1,192,8192]{2,1,0:T(8,128)(2,1)S(1)}, f32[192,512]{1,0:T(8,128)S(1)}) custom-call(bf16[1,192,8192]{2,1,0:T(8,128)(2,1)} %g.1, bf16[1,192,8192]{2,1,0:T(8,128)(2,1)} %e.1, bf16[192,512]{1,0:T(8,128)(2,1)} %b.1), custom_call_target="tpu_custom_call" | custom-call | tf_op jit(solution)/shard_map/exchange_step/pallas_call | solution.py:424
  72.2 0.0 copy-done.1
  72.2 0.0 copy-done
  72.2 1.0 %multiply_subtract_fusion = (f32[192,512]{1,0:T(8,128)}, f32[192,512]{1,0:T(8,128)}) fusion(f32[192,512]{1,0:T(8,128)S(1)} %copy-done, f32[192,512]{1,0:T(8,128)S(1)} %get-tuple-element.5, f32[192,512]{1,0:T(8,128)S(1)} %copy-done.1), kind=kLoop, calls=%fused_computation | loop fusion | flops 589824 | bytes 1966080 | tf_op jit(solution)/shard_map/sub | solution.py:470
  73.2 1.7 %copy.9 = bf16[1,192,8192]{2,1,0:T(8,128)(2,1)} copy(bf16[1,192,8192]{2,1,0:T(8,128)(2,1)S(1)} %get-tuple-element.14) | data formatting | bytes 6291456
Async XLA Ops:
  0.6 71.6 %copy-start.1 = (f32[192,512]{1,0:T(8,128)S(1)}, f32[192,512]{1,0:T(8,128)}, u32[]{:S(2)}) copy-start(f32[192,512]{1,0:T(8,128)} %param.9) | copy-start | bytes 1179652
  0.6 71.6 %copy-start = (f32[192,512]{1,0:T(8,128)S(1)}, f32[192,512]{1,0:T(8,128)}, u32[]{:S(2)}) copy-start(f32[192,512]{1,0:T(8,128)} %param.8) | copy-start | bytes 1179652
